TPU v7x, 32 devices: a whole 2x2x4 slice. The times are simulated.
32 devices in a mesh: dp: 8 (over z, y), ctx: 2 (over x), tensor: 2 (over core).
Axes of the slice: x: 2, y: 2, z: 4, core: 2. Of those that a mesh axis runs over, the one named last changes fastest.
Arguments:
- block_input: bfloat16 [8, 384, 1024], P('dp', 'ctx'), may hold values from -6 to 6
- attn_gain: float32 [1024], replicated, may hold values from 0.1 to 1.9
- query_weight: bfloat16 [1024, 2048], P('dp', 'tensor'), may hold values from -0.1875 to 0.1875
- key_weight: bfloat16 [1024, 1024], P('dp', 'tensor'), may hold values from -0.1875 to 0.1875
- value_weight: bfloat16 [1024, 1024], P('dp', 'tensor'), may hold values from -0.1875 to 0.1875
- query_gain: float32 [128], replicated, may hold values from 0.5 to 12
- key_gain: float32 [128], replicated, may hold values from 0.5 to 12
- output_weight: bfloat16 [2048, 1024], P('tensor', 'dp'), may hold values from -1 to 1
- mlp_gain: float32 [1024], replicated, may hold values from 0.1 to 1.9
- gate_weight: bfloat16 [1024, 3072], P('dp', 'tensor'), may hold values from -0.1875 to 0.1875
- up_weight: bfloat16 [1024, 3072], P('dp', 'tensor'), may hold values from -0.1875 to 0.1875
- down_weight: bfloat16 [3072, 1024], P('tensor', 'dp'), may hold values from -0.109375 to 0.109375
- cotangent: bfloat16 [8, 384, 1024], P('dp', 'ctx'), may hold values from -6 to 6
Outputs:
- block_output: bfloat16 [8, 384, 1024], P('dp', 'ctx')
- input_grad: bfloat16 [8, 384, 1024], P('dp', 'ctx')
- attn_gain_grad: float32 [1024], P('dp')
- query_weight_grad: float32 [1024, 2048], P('dp', 'tensor')
- key_weight_grad: float32 [1024, 1024], P('dp', 'tensor')
- value_weight_grad: float32 [1024, 1024], P('dp', 'tensor')
- query_gain_grad: float32 [128], P('dp')
- key_gain_grad: float32 [128], P('dp')
- output_weight_grad: float32 [2048, 1024], P('tensor', 'dp')
- mlp_gain_grad: float32 [1024], P('dp')
- gate_weight_grad: float32 [1024, 3072], P('dp', 'tensor')
- up_weight_grad: float32 [1024, 3072], P('dp', 'tensor')
- down_weight_grad: float32 [3072, 1024], P('tensor', 'dp')
All inputs are finite; a program needn't handle non-finite values.
Results may differ from a plain program's by a relative error of at most 0.015.
The roundings to bfloat16 on the way count: a program that leaves them out, or rounds other values in their place, can miss the bound.
Values may be sent and summed in bfloat16 or wider, within the bound.
A program may use at most 128 MiB of HBM per device.

v0:
```python
import math

import jax
import jax.numpy as jnp
from jax import lax
from jax.sharding import PartitionSpec as P

HD = 128


EPS = 1e-06
THETA = 1000000.0
F32 = jnp.float32
BF16 = jnp.bfloat16


def rms_inverse(value):
    return lax.rsqrt(jnp.mean(value * value, axis=-1, keepdims=True) + EPS)


def norm_back(grad, unit, inverse, gain):
    scaled = grad * gain
    return inverse * (scaled - unit * jnp.mean(scaled * unit, axis=-1, keepdims=True))


def rotate(value):
    half_width = value.shape[-1] // 2
    return jnp.concatenate([-value[..., half_width:], value[..., :half_width]], axis=-1)


def rotate_back(value):
    half_width = value.shape[-1] // 2
    return jnp.concatenate([value[..., half_width:], -value[..., :half_width]], axis=-1)


def rope_tables(positions, width):
    half_width = width // 2
    exponent = jnp.arange(half_width).astype(F32) * (2.0 / width)
    frequency = jnp.power(THETA, -exponent)
    angle = positions.astype(F32)[:, None] * frequency[None, :]
    angle = jnp.concatenate([angle, angle], axis=-1)
    return (jnp.cos(angle), jnp.sin(angle))


def over_heads(partial_value):
    return lax.psum(partial_value, "tensor")


def per_device(
    block_input,
    attn_gain,
    query_weight,
    key_weight,
    value_weight,
    query_gain,
    key_gain,
    output_weight,
    mlp_gain,
    gate_weight,
    up_weight,
    down_weight,
    cotangent,
):
    tokens = block_input[0].astype(F32)
    row_count = tokens.shape[0]
    score_scale = 1.0 / math.sqrt(HD)
    positions = lax.axis_index("ctx") * row_count + jnp.arange(row_count, dtype=jnp.int32)
    cos_table, sin_table = rope_tables(positions, HD)
    cos_heads = cos_table[:, None, :]
    sin_heads = sin_table[:, None, :]
    w_query, w_key, w_value, w_out, w_gate, w_up, w_down = (
        lax.all_gather(query_weight, "dp", axis=0, tiled=True),
        lax.all_gather(key_weight, "dp", axis=0, tiled=True),
        lax.all_gather(value_weight, "dp", axis=0, tiled=True),
        lax.all_gather(output_weight, "dp", axis=1, tiled=True),
        lax.all_gather(gate_weight, "dp", axis=0, tiled=True),
        lax.all_gather(up_weight, "dp", axis=0, tiled=True),
        lax.all_gather(down_weight, "dp", axis=1, tiled=True),
    )
    q_heads = w_query.shape[1] // HD
    kv_heads = w_key.shape[1] // HD
    group_size = q_heads // kv_heads
    inv_one = rms_inverse(tokens)
    unit_one = tokens * inv_one
    normed_one = (unit_one * attn_gain).astype(BF16)
    query = jnp.dot(normed_one, w_query, preferred_element_type=F32).reshape(row_count, q_heads, HD)
    key_raw = jnp.dot(normed_one, w_key, preferred_element_type=F32).reshape(
        row_count, kv_heads, HD
    )
    value = (
        jnp.dot(normed_one, w_value, preferred_element_type=F32)
        .astype(BF16)
        .reshape(row_count, kv_heads, HD)
    )
    query_inv = rms_inverse(query)
    query_unit = query * query_inv
    query_scaled = query_unit * query_gain
    query_rot = (query_scaled * cos_heads + rotate(query_scaled) * sin_heads).astype(BF16)
    key_inv = rms_inverse(key_raw)
    key_unit = key_raw * key_inv
    key_scaled = key_unit * key_gain
    key_rot = (key_scaled * cos_heads + rotate(key_scaled) * sin_heads).astype(BF16)
    grouped_query = query_rot.reshape(row_count, kv_heads, group_size, HD)

    def piece_scores(piece_keys):
        piece_rows = piece_keys.shape[0]
        key_positions = jnp.arange(piece_rows, dtype=jnp.int32)
        allowed = key_positions[None, :] <= positions[:, None]
        scores = (
            jnp.einsum("qkgd,nkd->kgqn", grouped_query, piece_keys, preferred_element_type=F32)
            * score_scale
        )
        return jnp.where(allowed, scores, -jnp.inf)

    peak_old = jnp.full((kv_heads, group_size, row_count), -1e30, F32)
    piece_keys = lax.all_gather(key_rot, "ctx", axis=0, tiled=True)
    piece_values = lax.all_gather(value, "ctx", axis=0, tiled=True)
    scores = piece_scores(piece_keys)
    peak_new = jnp.maximum(peak_old, jnp.max(scores, axis=-1))
    expo = jnp.exp(scores - peak_new[..., None])
    total_new = jnp.sum(expo, axis=-1)
    accum_new = jnp.einsum(
        "kgqn,nkd->kgqd", expo.astype(BF16), piece_values, preferred_element_type=F32
    )
    log_total = peak_new + jnp.log(total_new)
    attn = (
        (accum_new / total_new[..., None])
        .astype(BF16)
        .transpose(2, 0, 1, 3)
        .reshape(row_count, q_heads * HD)
    )
    resid = tokens + over_heads(jnp.dot(attn, w_out, preferred_element_type=F32))
    inv_two = rms_inverse(resid)
    unit_two = resid * inv_two
    normed_two = (unit_two * mlp_gain).astype(BF16)
    gate = jnp.dot(normed_two, w_gate, preferred_element_type=F32)
    up_proj = jnp.dot(normed_two, w_up, preferred_element_type=F32)
    sigma = jax.nn.sigmoid(gate)
    silu_gate = gate * sigma
    hidden = (silu_gate * up_proj).astype(BF16)
    output = (resid + over_heads(jnp.dot(hidden, w_down, preferred_element_type=F32))).astype(BF16)
    w_query, w_key, w_value, w_out, w_gate, w_up, w_down = (
        lax.all_gather(query_weight, "dp", axis=0, tiled=True),
        lax.all_gather(key_weight, "dp", axis=0, tiled=True),
        lax.all_gather(value_weight, "dp", axis=0, tiled=True),
        lax.all_gather(output_weight, "dp", axis=1, tiled=True),
        lax.all_gather(gate_weight, "dp", axis=0, tiled=True),
        lax.all_gather(up_weight, "dp", axis=0, tiled=True),
        lax.all_gather(down_weight, "dp", axis=1, tiled=True),
    )
    d_output = cotangent[0]
    d_hidden = jnp.einsum("td,fd->tf", d_output, w_down, preferred_element_type=F32)
    grad_down = jnp.einsum("tf,td->fd", hidden, d_output, preferred_element_type=F32)
    d_gate = (d_hidden * up_proj * sigma * (1.0 + gate * (1.0 - sigma))).astype(BF16)
    d_up = (d_hidden * silu_gate).astype(BF16)
    grad_gate = jnp.einsum("td,tf->df", normed_two, d_gate, preferred_element_type=F32)
    grad_up = jnp.einsum("td,tf->df", normed_two, d_up, preferred_element_type=F32)
    partial_two = jnp.einsum("tf,df->td", d_gate, w_gate, preferred_element_type=F32) + jnp.einsum(
        "tf,df->td", d_up, w_up, preferred_element_type=F32
    )
    d_normed_two = lax.psum(partial_two, "tensor")
    grad_mlp_gain = jnp.sum(d_normed_two * unit_two, axis=0)
    d_resid = d_output.astype(F32) + norm_back(d_normed_two, unit_two, inv_two, mlp_gain)
    d_resid_b = d_resid.astype(BF16)
    grad_out = jnp.einsum("th,td->hd", attn, d_resid_b, preferred_element_type=F32)
    d_attn = jnp.einsum("td,hd->th", d_resid_b, w_out, preferred_element_type=F32).astype(BF16)
    delta = jnp.sum(
        d_attn.astype(F32).reshape(row_count, q_heads, HD)
        * attn.astype(F32).reshape(row_count, q_heads, HD),
        axis=-1,
    )
    delta_heads = delta.reshape(row_count, kv_heads, group_size).transpose(1, 2, 0)
    grouped_grad = d_attn.reshape(row_count, kv_heads, group_size, HD)
    piece_keys = lax.all_gather(key_rot, "ctx", axis=0, tiled=True)
    piece_values = lax.all_gather(value, "ctx", axis=0, tiled=True)
    piece_rows = piece_keys.shape[0]
    scores = piece_scores(piece_keys)
    probs = jnp.exp(scores - log_total[..., None])
    d_probs = jnp.einsum("qkgd,nkd->kgqn", grouped_grad, piece_values, preferred_element_type=F32)
    d_scores = (probs * (d_probs - delta_heads[..., None]) * score_scale).astype(BF16)
    d_query_acc = jnp.einsum("kgqn,nkd->kgqd", d_scores, piece_keys, preferred_element_type=F32)
    d_key_piece = jnp.einsum("kgqn,qkgd->nkd", d_scores, grouped_query, preferred_element_type=F32)
    d_value_piece = jnp.einsum(
        "kgqn,qkgd->nkd", probs.astype(BF16), grouped_grad, preferred_element_type=F32
    )
    update = jnp.stack([d_key_piece, d_value_piece])
    d_kv_home = lax.psum_scatter(update, "ctx", scatter_dimension=1, tiled=True)
    d_query_rot = d_query_acc.transpose(2, 0, 1, 3).reshape(row_count, q_heads, HD)
    d_key_rot = d_kv_home[0]
    d_value = d_kv_home[1].astype(BF16).reshape(row_count, kv_heads * HD)
    d_query_scaled = d_query_rot * cos_heads + rotate_back(d_query_rot * sin_heads)
    d_key_scaled = d_key_rot * cos_heads + rotate_back(d_key_rot * sin_heads)
    query_gain_part = jnp.sum(d_query_scaled * query_unit, axis=(0, 1))
    key_gain_part = jnp.sum(d_key_scaled * key_unit, axis=(0, 1))
    d_query = (
        norm_back(d_query_scaled, query_unit, query_inv, query_gain)
        .astype(BF16)
        .reshape(row_count, q_heads * HD)
    )
    d_key = (
        norm_back(d_key_scaled, key_unit, key_inv, key_gain)
        .astype(BF16)
        .reshape(row_count, kv_heads * HD)
    )
    grad_query = jnp.einsum("td,th->dh", normed_one, d_query, preferred_element_type=F32)
    grad_key = jnp.einsum("td,th->dh", normed_one, d_key, preferred_element_type=F32)
    grad_value = jnp.einsum("td,th->dh", normed_one, d_value, preferred_element_type=F32)
    partial_one = jnp.einsum("th,dh->td", d_query, w_query, preferred_element_type=F32)
    partial_one = partial_one + jnp.einsum("th,dh->td", d_key, w_key, preferred_element_type=F32)
    partial_one = partial_one + jnp.einsum(
        "th,dh->td", d_value, w_value, preferred_element_type=F32
    )
    d_normed_one, query_gain_heads, key_gain_heads = lax.psum(
        (partial_one, query_gain_part, key_gain_part), "tensor"
    )
    grad_attn_gain = jnp.sum(d_normed_one * unit_one, axis=0)
    d_input = (d_resid + norm_back(d_normed_one, unit_one, inv_one, attn_gain)).astype(BF16)
    (
        share_a,
        share_q,
        share_k,
        share_v,
        share_qg,
        share_kg,
        share_o,
        share_m,
        share_g,
        share_u,
        share_d,
    ) = (
        lax.psum_scatter(grad_attn_gain, "dp", scatter_dimension=0, tiled=True),
        lax.psum_scatter(grad_query, "dp", scatter_dimension=0, tiled=True),
        lax.psum_scatter(grad_key, "dp", scatter_dimension=0, tiled=True),
        lax.psum_scatter(grad_value, "dp", scatter_dimension=0, tiled=True),
        lax.psum_scatter(query_gain_heads, "dp", scatter_dimension=0, tiled=True),
        lax.psum_scatter(key_gain_heads, "dp", scatter_dimension=0, tiled=True),
        lax.psum_scatter(grad_out, "dp", scatter_dimension=1, tiled=True),
        lax.psum_scatter(grad_mlp_gain, "dp", scatter_dimension=0, tiled=True),
        lax.psum_scatter(grad_gate, "dp", scatter_dimension=0, tiled=True),
        lax.psum_scatter(grad_up, "dp", scatter_dimension=0, tiled=True),
        lax.psum_scatter(grad_down, "dp", scatter_dimension=1, tiled=True),
    )
    finals = lax.psum(
        (
            share_a,
            share_q,
            share_k,
            share_v,
            share_qg,
            share_kg,
            share_o,
            share_m,
            share_g,
            share_u,
            share_d,
        ),
        "ctx",
    )
    return (
        output[None],
        d_input[None],
        finals[0],
        finals[1],
        finals[2],
        finals[3],
        finals[4],
        finals[5],
        finals[6],
        finals[7],
        finals[8],
        finals[9],
        finals[10],
    )


def solution(mesh):
    return jax.shard_map(
        per_device,
        mesh=mesh,
        in_specs=(
            P("dp", "ctx", None),
            P(),
            P("dp", "tensor"),
            P("dp", "tensor"),
            P("dp", "tensor"),
            P(),
            P(),
            P("tensor", "dp"),
            P(),
            P("dp", "tensor"),
            P("dp", "tensor"),
            P("tensor", "dp"),
            P("dp", "ctx", None),
        ),
        out_specs=(
            P("dp", "ctx", None),
            P("dp", "ctx", None),
            P("dp"),
            P("dp", "tensor"),
            P("dp", "tensor"),
            P("dp", "tensor"),
            P("dp"),
            P("dp"),
            P("tensor", "dp"),
            P("dp"),
            P("dp", "tensor"),
            P("dp", "tensor"),
            P("tensor", "dp"),
        ),
        check_vma=False,
    )
```

profile of v0, /device:TPU:0, one launch (start us, length us, event | category | flops | bytes accessed | tf_op | source)
XLA Modules:
  0.0 1308.8 jit_solution(13740826629535739821)
XLA Ops:
  12.5 40.6 %all-gather.12.cloned.1.call-done = bf16[1024,512]{1,0:T(8,128)(2,1)} async-done(((bf16[128,512]{1,0:T(8,128)(2,1)}), bf16[1024,512]{1,0:T(8,128)(2,1)}) %all-gather.12.cloned.1.call-update) | async-done | bytes 1048592 | tf_op jit(solution)/shard_map/all_gather | solution.py:74
  55.0 6.4 all_gather.40
  61.4 32.9 %all-gather.8.cloned.1.call-done = bf16[1024,512]{1,0:T(8,128)(2,1)} async-done(((bf16[128,512]{1,0:T(8,128)(2,1)}), bf16[1024,512]{1,0:T(8,128)(2,1)}) %all-gather.8.cloned.1.call-update) | async-done | bytes 1048592 | tf_op jit(solution)/shard_map/all_gather | solution.py:73
  97.2 6.4 all_gather.37
  103.6 40.6 %all-gather.10.cloned.1.call-done = bf16[1024,1024]{1,0:T(8,128)(2,1)} async-done(((bf16[128,1024]{1,0:T(8,128)(2,1)}), bf16[1024,1024]{1,0:T(8,128)(2,1)}) %all-gather.10.cloned.1.call-update) | async-done | bytes 2097168 | tf_op jit(solution)/shard_map/all_gather | solution.py:72
  154.8 40.2 %all-gather.14.cloned.1.call-done = bf16[1024,1024]{1,0:T(8,128)(2,1)} async-done(((bf16[1024,128]{1,0:T(8,128)(2,1)}), bf16[1024,1024]{1,0:T(8,128)(2,1)}) %all-gather.14.cloned.1.call-update) | async-done | bytes 2097168 | tf_op jit(solution)/shard_map/all_gather | solution.py:75
  195.1 3.0 fusion.93
  200.4 15.0 %all-reduce.14.cloned.1.call-done = f32[192,1024]{1,0:T(8,128)} async-done(((f32[192,1024]{1,0:T(8,128)}), f32[192,1024]{1,0:T(8,128)}) %all-reduce.14.cloned.1.call-update) | async-done | bytes 786448 | tf_op jit(solution)/shard_map/psum | solution.py:46
  218.9 59.8 %all-gather.18.cloned.1.call-done = bf16[1024,1536]{1,0:T(8,128)(2,1)} async-done(((bf16[128,1536]{1,0:T(8,128)(2,1)}), bf16[1024,1536]{1,0:T(8,128)(2,1)}) %all-gather.18.cloned.1.call-update) | async-done | bytes 3145744 | tf_op jit(solution)/shard_map/all_gather | solution.py:77
  278.7 3.8 fusion.95
  282.6 57.1 %all-gather.16.cloned.1.call-done = bf16[1024,1536]{1,0:T(8,128)(2,1)} async-done(((bf16[128,1536]{1,0:T(8,128)(2,1)}), bf16[1024,1536]{1,0:T(8,128)(2,1)}) %all-gather.16.cloned.1.call-update) | async-done | bytes 3145744 | tf_op jit(solution)/shard_map/all_gather | solution.py:76
  339.6 3.8 fusion.94
  343.4 59.6 %all-gather.20.cloned.1.call-done = bf16[1536,1024]{1,0:T(8,128)(2,1)} async-done(((bf16[1536,128]{1,0:T(8,128)(2,1)}), bf16[1536,1024]{1,0:T(8,128)(2,1)}) %all-gather.20.cloned.1.call-update) | async-done | bytes 3145744 | tf_op jit(solution)/shard_map/all_gather | solution.py:78
  403.0 5.2 multiply_convert_fusion
  413.9 15.9 %all-reduce.16.cloned.1.call-done = f32[192,1024]{1,0:T(8,128)} async-done(((f32[192,1024]{1,0:T(8,128)}), f32[192,1024]{1,0:T(8,128)}) %all-reduce.16.cloned.1.call-update) | async-done | bytes 786448 | tf_op jit(solution)/shard_map/psum | solution.py:161
  447.3 27.5 %reduce-scatter.9.cloned.1.call-done = f32[2,192,4,128]{3,1,2,0:T(8,128)} async-done(((f32[2,384,4,128]{3,1,2,0:T(8,128)}), f32[2,192,4,128]{3,1,2,0:T(8,128)}) %reduce-scatter.9.cloned.1.call-update) | async-done | bytes 786448 | tf_op jit(solution)/shard_map/reduce_scatter | solution.py:187
  490.9 2.9 fusion.38
  495.0 3.7 fusion.49
  499.7 4.8 fusion.99
  504.6 4.7 fusion.98
  509.4 3.8 fusion.96
  516.4 30.7 %reduce-scatter.15.cloned.1.call-done = f32[128,512]{1,0:T(8,128)} async-done(((f32[1024,512]{1,0:T(8,128)}), f32[128,512]{1,0:T(8,128)}) %reduce-scatter.15.cloned.1.call-update) | async-done | bytes 262160 | tf_op jit(solution)/shard_map/reduce_scatter | solution.py:234
  547.1 70.8 %reduce-scatter.13.cloned.1.call-done = f32[128,512]{1,0:T(8,128)} async-done(((f32[1024,512]{1,0:T(8,128)}), f32[128,512]{1,0:T(8,128)}) %reduce-scatter.13.cloned.1.call-update) | async-done | bytes 262160 | tf_op jit(solution)/shard_map/reduce_scatter | solution.py:233
  617.9 91.4 %reduce-scatter.17.cloned.1.call-done = f32[1024,128]{1,0:T(8,128)} async-done(((f32[1024,1024]{1,0:T(8,128)}), f32[1024,128]{1,0:T(8,128)}) %reduce-scatter.17.cloned.1.call-update) | async-done | bytes 524304 | tf_op jit(solution)/shard_map/reduce_scatter | solution.py:237
  709.2 91.5 %reduce-scatter.11.cloned.1.call-done = f32[128,1024]{1,0:T(8,128)} async-done(((f32[1024,1024]{1,0:T(8,128)}), f32[128,1024]{1,0:T(8,128)}) %reduce-scatter.11.cloned.1.call-update) | async-done | bytes 524304 | tf_op jit(solution)/shard_map/reduce_scatter | solution.py:232
  800.7 121.6 %reduce-scatter.23.cloned.1.call-done = f32[1536,128]{1,0:T(8,128)} async-done(((f32[1536,1024]{1,0:T(8,128)}), f32[1536,128]{1,0:T(8,128)}) %reduce-scatter.23.cloned.1.call-update) | async-done | bytes 786448 | tf_op jit(solution)/shard_map/reduce_scatter | solution.py:241
  922.3 120.8 %reduce-scatter.21.cloned.1.call-done = f32[128,1536]{1,0:T(8,128)} async-done(((f32[1024,1536]{1,0:T(8,128)}), f32[128,1536]{1,0:T(8,128)}) %reduce-scatter.21.cloned.1.call-update) | async-done | bytes 786448 | tf_op jit(solution)/shard_map/reduce_scatter | solution.py:240
  1043.1 120.8 %reduce-scatter.19.cloned.1.call-done = f32[128,1536]{1,0:T(8,128)} async-done(((f32[1024,1536]{1,0:T(8,128)}), f32[128,1536]{1,0:T(8,128)}) %reduce-scatter.19.cloned.1.call-update) | async-done | bytes 786448 | tf_op jit(solution)/shard_map/reduce_scatter | solution.py:239
  1165.8 20.6 %all-reduce.18.cloned.1.call-done = (f32[192,1024]{1,0:T(8,128)}, f32[192,1024]{1,0:T(8,128)}) async-done(((f32[192,1024]{1,0:T(8,128)}, f32[192,1024]{1,0:T(8,128)}), (f32[192,1024]{1,0:T(8,128)}, f32[192,1024]{1,0:T(8,128)})) %all-reduce.18.cloned.1.call-update) | async-done | bytes 1572880 | tf_op jit(solution)/shard_map/psum | solution.py:46
  1187.9 22.1 %all-reduce.4 = (f32[1024]{0:T(1024)S(1)}, f32[128]{0:T(128)S(1)}, f32[128]{0:T(128)S(1)}, f32[1024]{0:T(1024)S(1)}) all-reduce(f32[1024]{0:T(1024)S(1)} %get-tuple-element.17, f32[128]{0:T(128)S(1)} %get-tuple-element.13, f32[128]{0:T(128)S(1)} %copy-done.60, ...), channel_id=3, replica_groups=mesh['dp'=8,'ctx'=2,'tensor'=2] {'dp'}, use_global_device_ids=true, to_apply=%region_17.18.clone | all-reduce | flops 2304 | bytes 18432
  1212.8 5.6 all-reduce.7
  1220.9 72.5 %all-reduce.20.cloned.1.call-done = (f32[128,1024]{1,0:T(8,128)}, f32[128,512]{1,0:T(8,128)}, f32[128,512]{1,0:T(8,128)}, f32[1024,128]{1,0:T(8,128)}, f32[128,1...) async-done(((f32[128,1024]{1,0:T(8,128)}, f32[128,512]{1,0:T(8,128)}, f32[128,512]{1,0:T(8,128)}, f32[1024,128]{1,0:T(8,128)}, f32[128,1536]{1,0:T(8,128)}, ...) | async-done | bytes 3932176 | tf_op jit(solution)/shard_map/psum | solution.py:243
  (243 shorter events, 86.7 us)
Async XLA Ops:
  7.2 46.0 %all-gather.12.cloned.1.call-start = ((), (), s32[]{:S(2)}) async-start(), calls=%async_computation.10 | async-start | bytes 1179648 | tf_op jit(solution)/shard_map/all_gather | solution.py:74
  7.9 86.4 %all-gather.8.cloned.1.call-start = ((), (), s32[]{:S(2)}) async-start(), calls=%async_computation.8 | async-start | bytes 1179648 | tf_op jit(solution)/shard_map/all_gather | solution.py:73
  8.7 135.6 %all-gather.10.cloned.1.call-start = ((), (), s32[]{:S(2)}) async-start(), calls=%async_computation.9 | async-start | bytes 2359296 | tf_op jit(solution)/shard_map/all_gather | solution.py:72
  9.4 185.7 %all-gather.14.cloned.1.call-start = ((), (), s32[]{:S(2)}) async-start(), calls=%async_computation.11 | async-start | bytes 2359296 | tf_op jit(solution)/shard_map/all_gather | solution.py:75
  10.0 205.5 %all-reduce.14.cloned.1.call-start = ((), (), s32[]{:S(2)}) async-start(), calls=%async_computation.12 | async-start | bytes 1572864 | tf_op jit(solution)/shard_map/psum | solution.py:46
  11.2 135.9 %copy-start.49 = (f32[192]{0:T(256)}, f32[192]{0:T(256)S(1)}, u32[]{:S(2)}) copy-start(f32[192]{0:T(256)S(1)} %add_rsqrt_fusion.3) | copy-start | bytes 2308
  12.5 136.3 %copy-start.23 = (f32[192,128]{1,0:T(8,128)}, f32[192,128]{1,0:T(8,128)S(1)}, u32[]{:S(2)}) copy-start(f32[192,128]{1,0:T(8,128)S(1)} %get-tuple-element.54) | copy-start | bytes 294916
  12.5 136.3 %copy-start.26 = (f32[192,128]{1,0:T(8,128)}, f32[192,128]{1,0:T(8,128)S(1)}, u32[]{:S(2)}) copy-start(f32[192,128]{1,0:T(8,128)S(1)} %get-tuple-element.55) | copy-start | bytes 294916
  12.5 83.3 %copy-start = (bf16[1,192,1024]{2,1,0:T(8,128)(2,1)S(1)}, bf16[1,192,1024]{2,1,0:T(8,128)(2,1)}, u32[]{:S(2)}) copy-start(bf16[1,192,1024]{2,1,0:T(8,128)(2,1)} %param.13) | copy-start | bytes 1179652
  12.5 83.3 %copy-start.46 = (f32[1024]{0:T(1024)S(1)}, f32[1024]{0:T(1024)}, u32[]{:S(2)}) copy-start(f32[1024]{0:T(1024)} %param.14) | copy-start | bytes 12292
  55.0 41.5 %copy-start.56 = (f32[128]{0:T(128)S(1)}, f32[128]{0:T(128)}, u32[]{:S(2)}) copy-start(f32[128]{0:T(128)} %param.19) | copy-start | bytes 1540
  96.5 50.6 %copy-start.12 = (f32[192,4,128]{2,0,1:T(8,128)}, f32[192,4,128]{2,0,1:T(8,128)S(1)}, u32[]{:S(2)}) copy-start(f32[192,4,128]{2,0,1:T(8,128)S(1)} %get-tuple-element.59) | copy-start | bytes 1179652
  152.4 45.7 %copy-start.37 = (bf16[192,4,2,128]{3,0,2,1:T(8,128)(2,1)}, bf16[192,4,2,128]{3,0,2,1:T(8,128)(2,1)S(1)}, u32[]{:S(2)}) copy-start(bf16[192,4,2,128]{3,0,2,1:T(8,128)(2,1)S(1)} %fusion.7) | copy-start | bytes 1179652
  154.8 44.6 %copy-start.21 = (bf16[192,1024]{1,0:T(8,128)(2,1)}, bf16[192,1024]{1,0:T(8,128)(2,1)S(1)}, u32[]{:S(2)}) copy-start(bf16[192,1024]{1,0:T(8,128)(2,1)S(1)} %reshape.265) | copy-start | bytes 1179652
  198.1 80.6 %all-gather.18.cloned.1.call-start = ((), (), s32[]{:S(2)}) async-start(), calls=%async_computation.14 | async-start | bytes 3538944 | tf_op jit(solution)/shard_map/all_gather | solution.py:77
  198.7 140.9 %all-gather.16.cloned.1.call-start = ((), (), s32[]{:S(2)}) async-start(), calls=%async_computation.13 | async-start | bytes 3538944 | tf_op jit(solution)/shard_map/all_gather | solution.py:76
  199.5 203.5 %all-gather.20.cloned.1.call-start = ((), (), s32[]{:S(2)}) async-start(), calls=%async_computation.15 | async-start | bytes 3538944 | tf_op jit(solution)/shard_map/all_gather | solution.py:78
  200.2 229.7 %all-reduce.16.cloned.1.call-start = ((), (), s32[]{:S(2)}) async-start(), calls=%async_computation.16 | async-start | bytes 1572864 | tf_op jit(solution)/shard_map/psum | solution.py:161
  412.6 62.2 %reduce-scatter.9.cloned.1.call-start = ((), (), s32[]{:S(2)}) async-start(), calls=%async_computation.17 | async-start | bytes 2359296 | tf_op jit(solution)/shard_map/reduce_scatter | solution.py:187
  445.9 30.7 %copy-start.50 = (f32[192]{0:T(256)S(1)}, f32[192]{0:T(256)}, u32[]{:S(2)}) copy-start(f32[192]{0:T(256)} %copy-done.49) | copy-start | bytes 2308
  447.3 99.8 %reduce-scatter.15.cloned.1.call-start = ((), (), s32[]{:S(2)}) async-start(), calls=%async_computation.20 | async-start | bytes 2359296 | tf_op jit(solution)/shard_map/reduce_scatter | solution.py:234
  478.5 139.3 %reduce-scatter.13.cloned.1.call-start = ((), (), s32[]{:S(2)}) async-start(), calls=%async_computation.19 | async-start | bytes 2359296 | tf_op jit(solution)/shard_map/reduce_scatter | solution.py:233
  483.2 226.0 %reduce-scatter.17.cloned.1.call-start = ((), (), s32[]{:S(2)}) async-start(), calls=%async_computation.21 | async-start | bytes 4718592 | tf_op jit(solution)/shard_map/reduce_scatter | solution.py:237
  486.1 314.6 %reduce-scatter.11.cloned.1.call-start = ((), (), s32[]{:S(2)}) async-start(), calls=%async_computation.18 | async-start | bytes 4718592 | tf_op jit(solution)/shard_map/reduce_scatter | solution.py:232
  493.9 428.4 %reduce-scatter.23.cloned.1.call-start = ((), (), s32[]{:S(2)}) async-start(), calls=%async_computation.24 | async-start | bytes 7077888 | tf_op jit(solution)/shard_map/reduce_scatter | solution.py:241
  498.7 544.3 %reduce-scatter.21.cloned.1.call-start = ((), (), s32[]{:S(2)}) async-start(), calls=%async_computation.23 | async-start | bytes 7077888 | tf_op jit(solution)/shard_map/reduce_scatter | solution.py:240
  504.5 659.3 %reduce-scatter.19.cloned.1.call-start = ((), (), s32[]{:S(2)}) async-start(), calls=%async_computation.22 | async-start | bytes 7077888 | tf_op jit(solution)/shard_map/reduce_scatter | solution.py:239
  509.3 677.1 %all-reduce.18.cloned.1.call-start = ((), (), s32[]{:S(2)}) async-start(), calls=%async_computation.25 | async-start | bytes 3145728 | tf_op jit(solution)/shard_map/psum | solution.py:46
  516.3 647.6 %copy-start.61 = (u32[32]{0:T(128)S(1)}, u32[32]{0:T(128)}, u32[]{:S(2)}) copy-start(u32[32]{0:T(128)} %constant.41) | copy-start | bytes 388
  516.3 777.0 %all-reduce.20.cloned.1.call-start = ((), (), s32[]{:S(2)}) async-start(), calls=%async_computation.26 | async-start | bytes 7864320 | tf_op jit(solution)/shard_map/psum | solution.py:243
  1163.8 24.0 %copy-start.54 = (f32[1024]{0:T(1024)S(1)}, f32[1024]{0:T(1024)}, u32[]{:S(2)}) copy-start(f32[1024]{0:T(1024)} %get-tuple-element.15) | copy-start | bytes 12292
  1163.8 24.0 %copy-start.60 = (f32[128]{0:T(128)S(1)}, f32[128]{0:T(128)}, u32[]{:S(2)}) copy-start(f32[128]{0:T(128)} %get-tuple-element.19) | copy-start | bytes 1540
  (49 other events, 92.4 us)
Sparse Core Ops, SparseCore 0:
  10.1 42.9 all-gather.11
  55.3 38.9 all-gather.7
  96.4 47.7 all-gather.9
  146.2 48.8 all-gather.13
  198.3 17.1 all-reduce.13
  217.5 61.2 all-gather.17
  280.9 58.6 all-gather.15
  341.7 61.2 all-gather.19
  412.7 17.1 all-reduce.15
  447.4 27.3 reduce-scatter.8
  478.6 68.3 reduce-scatter.14
  550.4 67.3 reduce-scatter.12
  621.5 87.7 reduce-scatter.16
  712.7 87.9 reduce-scatter.10
  804.2 118.0 reduce-scatter.22
  925.7 117.2 reduce-scatter.20
  1046.5 117.2 reduce-scatter.18
  1166.6 19.6 all-reduce.17
  1189.1 104.2 all-reduce.19
where the time goes:
time: 1310 us
  waiting for transfers between devices  1130 us (86%)
  matrix products  58.3 us (4%)
  blocking collectives  43.1 us (3%)
  local copies, waits for them, and re-layouts  32.6 us (2%)
  other arithmetic  23.1 us (2%)
  between operations  16.1 us (1%)
    reduce_scatter x1, waiting for transfers between devices, per_device(): lax.psum_scatter(grad_down, 'dp', scatter_dimension=1, tiled=True)  122 us
    reduce_scatter x1, waiting for transfers between devices, per_device(): lax.psum_scatter(grad_up, 'dp', scatter_dimension=0, tiled=True)  121 us
    reduce_scatter x1, waiting for transfers between devices, per_device(): lax.psum_scatter(grad_gate, 'dp', scatter_dimension=0, tiled=True)  121 us
    reduce_scatter x1, waiting for transfers between devices, per_device(): lax.psum_scatter(grad_query, 'dp', scatter_dimension=0, tiled=True)  91.5 us
    reduce_scatter x1, waiting for transfers between devices, per_device(): lax.psum_scatter(grad_out, 'dp', scatter_dimension=1, tiled=True)  91.4 us
    psum x1, waiting for transfers between devices, per_device(): lax.psum((share_a, share_q, share_k, share_v, share_qg, share_kg, share_o...  72.5 us
    reduce_scatter x1, waiting for transfers between devices, per_device(): lax.psum_scatter(grad_key, 'dp', scatter_dimension=0, tiled=True)  70.8 us
    all_gather x1, waiting for transfers between devices, per_device(): lax.all_gather(up_weight, 'dp', axis=0, tiled=True)  59.8 us
  transfers between devices with their start and end apart: 19, of which 19 were waited for; matrix products, arithmetic and copies ran while one was open for 5% of the time, Pallas kernels for 0%

commit v1 on v0

--- a/solution.py
+++ b/solution.py
@@ -1,3 +1,4 @@
+import functools
 import math
 
 import jax
@@ -273,9 +274,305 @@
     )
 
 
+def tree_exchange(value, axis_name, axis_size):
+    return lax.ppermute(value, axis_name, [(i, i ^ 1) for i in range(axis_size)])
+
+
+def paired_device(
+    dp_size,
+    block_input,
+    attn_gain,
+    query_weight,
+    key_weight,
+    value_weight,
+    query_gain,
+    key_gain,
+    output_weight,
+    mlp_gain,
+    gate_weight,
+    up_weight,
+    down_weight,
+    cotangent,
+):
+    line = dp_size // 2
+    line_groups = [[2 * j + side for j in range(line)] for side in range(2)]
+    side = lax.axis_index("dp") % 2
+    block = lax.axis_index("ctx")
+    owned = query_weight.shape[0]
+    width = owned * dp_size
+
+    def to_ctx(value):
+        return tree_exchange(value, "ctx", 2)
+
+    def to_pair(value):
+        return tree_exchange(value, "dp", dp_size)
+
+    def over_tensor(value):
+        return value + tree_exchange(value, "tensor", 2)
+
+    def to_local(value):
+        split = value.reshape(value.shape[:-1] + (line, 2, owned))
+        first, second = split[..., 0, :], split[..., 1, :]
+        ordered = jnp.where(
+            side == 0,
+            jnp.stack([first, second], axis=-3),
+            jnp.stack([second, first], axis=-3),
+        )
+        return ordered.reshape(value.shape)
+
+    def from_local(value):
+        split = value.reshape(value.shape[:-1] + (2, line, owned))
+        first, second = split[..., 0, :, :], split[..., 1, :, :]
+        ordered = jnp.where(
+            side == 0,
+            jnp.stack([first, second], axis=-2),
+            jnp.stack([second, first], axis=-2),
+        )
+        return ordered.reshape(value.shape)
+
+    def own_half(shard):
+        half = shard.shape[1] // 2
+        return lax.dynamic_slice_in_dim(shard, block * half, half, axis=1)
+
+    def gather_line(shard):
+        return lax.all_gather(
+            shard, "dp", axis_index_groups=line_groups, axis=0, tiled=True
+        )
+
+    def spread_pair_first(part):
+        part = jnp.concatenate([part, to_pair(part)], axis=0)
+        return part, to_ctx(part)
+
+    def spread_ctx_first(part):
+        other = to_ctx(part)
+        return (
+            jnp.concatenate([part, to_pair(part)], axis=0),
+            jnp.concatenate([other, to_pair(other)], axis=0),
+        )
+
+    halves = [own_half(shard) for shard in (query_weight, key_weight, value_weight)]
+    cut_q = halves[0].shape[1]
+    cut_k = cut_q + halves[1].shape[1]
+    own_qkv, other_qkv = spread_pair_first(gather_line(jnp.concatenate(halves, axis=1)))
+
+    def both(low, high):
+        return jnp.concatenate([own_qkv[:, low:high], other_qkv[:, low:high]], axis=1)
+
+    w_query, w_key, w_value = both(0, cut_q), both(cut_q, cut_k), both(cut_k, own_qkv.shape[1])
+    w_out_t = jnp.concatenate(
+        spread_ctx_first(gather_line(own_half(output_weight.T))), axis=1
+    )
+    w_gate = jnp.concatenate(spread_ctx_first(gather_line(own_half(gate_weight))), axis=1)
+    w_up = jnp.concatenate(spread_pair_first(gather_line(own_half(up_weight))), axis=1)
+    w_down_t = jnp.concatenate(spread_ctx_first(gather_line(own_half(down_weight.T))), axis=1)
+
+    def both_blocks(value):
+        half = value.shape[1] // 2
+        return jnp.concatenate([value[:, :half], to_ctx(value[:, half:])], axis=0)
+
+    def feature_side(value):
+        value = jnp.concatenate([value, to_ctx(value)], axis=0)
+        half = value.shape[1] // 2
+        return jnp.concatenate([value[:, :half], to_pair(value[:, half:])], axis=0)
+
+    def column_side(value):
+        value = both_blocks(value)
+        return jnp.concatenate([value, to_pair(value)], axis=0)
+
+    def weight_share(features, columns):
+        part = jnp.einsum("td,tf->df", features, columns, preferred_element_type=F32)
+        share = lax.psum_scatter(
+            part, "dp", axis_index_groups=line_groups, scatter_dimension=0, tiled=True
+        )
+        return share, to_ctx(share)
+
+    def whole(share, other):
+        return jnp.where(
+            block == 0,
+            jnp.concatenate([share, other], axis=1),
+            jnp.concatenate([other, share], axis=1),
+        )
+
+    def mul_t(value, weight):
+        return jnp.einsum("tf,df->td", value, weight, preferred_element_type=F32)
+
+    row_count = block_input.shape[1]
+    score_scale = 1.0 / math.sqrt(HD)
+    attn_gain = to_local(attn_gain)
+    mlp_gain = to_local(mlp_gain)
+    tokens = to_local(block_input[0]).astype(F32)
+    d_output = to_local(cotangent[0])
+    positions = block * row_count + jnp.arange(row_count, dtype=jnp.int32)
+    other_positions = (1 - block) * row_count + jnp.arange(row_count, dtype=jnp.int32)
+    cos_table, sin_table = rope_tables(positions, HD)
+    cos_heads = cos_table[:, None, :]
+    sin_heads = sin_table[:, None, :]
+    q_heads = w_query.shape[1] // HD
+    kv_heads = w_key.shape[1] // HD
+    group_size = q_heads // kv_heads
+
+    inv_one = rms_inverse(tokens)
+    unit_one = tokens * inv_one
+    normed_one = (unit_one * attn_gain).astype(BF16)
+    query = jnp.dot(normed_one, w_query, preferred_element_type=F32).reshape(row_count, q_heads, HD)
+    key_raw = jnp.dot(normed_one, w_key, preferred_element_type=F32).reshape(
+        row_count, kv_heads, HD
+    )
+    value = (
+        jnp.dot(normed_one, w_value, preferred_element_type=F32)
+        .astype(BF16)
+        .reshape(row_count, kv_heads, HD)
+    )
+    query_inv = rms_inverse(query)
+    query_unit = query * query_inv
+    query_scaled = query_unit * query_gain
+    query_rot = (query_scaled * cos_heads + rotate(query_scaled) * sin_heads).astype(BF16)
+    key_inv = rms_inverse(key_raw)
+    key_unit = key_raw * key_inv
+    key_scaled = key_unit * key_gain
+    key_rot = (key_scaled * cos_heads + rotate(key_scaled) * sin_heads).astype(BF16)
+    grouped_query = query_rot.reshape(row_count, kv_heads, group_size, HD)
+
+    def swap_heads(array):
+        half = array.shape[-2] // 2
+        return jnp.concatenate([array[..., half:, :], array[..., :half, :]], axis=-2)
+
+    other_keys = swap_heads(to_ctx(key_rot))
+    other_values = swap_heads(to_ctx(value))
+    all_keys = jnp.concatenate([key_rot, other_keys], axis=0)
+    all_values = jnp.concatenate([value, other_values], axis=0)
+    key_positions = jnp.concatenate([positions, other_positions])
+    allowed = key_positions[None, :] <= positions[:, None]
+    scores = (
+        jnp.einsum("qkgd,nkd->kgqn", grouped_query, all_keys, preferred_element_type=F32)
+        * score_scale
+    )
+    scores = jnp.where(allowed, scores, -jnp.inf)
+    peak = jnp.max(scores, axis=-1)
+    expo = jnp.exp(scores - peak[..., None])
+    total = jnp.sum(expo, axis=-1)
+    accum = jnp.einsum("kgqn,nkd->kgqd", expo.astype(BF16), all_values, preferred_element_type=F32)
+    log_total = peak + jnp.log(total)
+    attn = (
+        (accum / total[..., None])
+        .astype(BF16)
+        .transpose(2, 0, 1, 3)
+        .reshape(row_count, q_heads * HD)
+    )
+    resid = tokens + over_tensor(mul_t(attn, w_out_t))
+    inv_two = rms_inverse(resid)
+    unit_two = resid * inv_two
+    normed_two = (unit_two * mlp_gain).astype(BF16)
+    gate = jnp.dot(normed_two, w_gate, preferred_element_type=F32)
+    up_proj = jnp.dot(normed_two, w_up, preferred_element_type=F32)
+    sigma = jax.nn.sigmoid(gate)
+    silu_gate = gate * sigma
+    hidden = (silu_gate * up_proj).astype(BF16)
+    output = from_local((resid + over_tensor(mul_t(hidden, w_down_t))).astype(BF16))
+
+    share_down = weight_share(feature_side(d_output), column_side(hidden))
+    d_hidden = jnp.dot(d_output, w_down_t, preferred_element_type=F32)
+    d_gate = (d_hidden * up_proj * sigma * (1.0 + gate * (1.0 - sigma))).astype(BF16)
+    d_up = (d_hidden * silu_gate).astype(BF16)
+    features_two = feature_side(normed_two)
+    share_gate = weight_share(features_two, column_side(d_gate))
+    share_up = weight_share(features_two, column_side(d_up))
+    d_normed_two = over_tensor(mul_t(d_gate, w_gate) + mul_t(d_up, w_up))
+    grad_mlp_gain = jnp.sum(d_normed_two * unit_two, axis=0)
+    d_resid = d_output.astype(F32) + norm_back(d_normed_two, unit_two, inv_two, mlp_gain)
+    d_resid_b = d_resid.astype(BF16)
+    share_out = weight_share(feature_side(d_resid_b), column_side(attn))
+    d_attn = jnp.dot(d_resid_b, w_out_t, preferred_element_type=F32).astype(BF16)
+    delta = jnp.sum(
+        d_attn.astype(F32).reshape(row_count, q_heads, HD)
+        * attn.astype(F32).reshape(row_count, q_heads, HD),
+        axis=-1,
+    )
+    delta_heads = delta.reshape(row_count, kv_heads, group_size).transpose(1, 2, 0)
+    grouped_grad = d_attn.reshape(row_count, kv_heads, group_size, HD)
+    probs = jnp.exp(scores - log_total[..., None])
+    d_probs = jnp.einsum("qkgd,nkd->kgqn", grouped_grad, all_values, preferred_element_type=F32)
+    d_scores = (probs * (d_probs - delta_heads[..., None]) * score_scale).astype(BF16)
+    d_query_acc = jnp.einsum("kgqn,nkd->kgqd", d_scores, all_keys, preferred_element_type=F32)
+    d_keys = jnp.einsum("kgqn,qkgd->nkd", d_scores, grouped_query, preferred_element_type=F32)
+    d_values = jnp.einsum(
+        "kgqn,qkgd->nkd", probs.astype(BF16), grouped_grad, preferred_element_type=F32
+    )
+    d_key_rot = d_keys[:row_count] + swap_heads(to_ctx(d_keys[row_count:]))
+    d_value_sum = d_values[:row_count] + swap_heads(to_ctx(d_values[row_count:]))
+    d_query_rot = d_query_acc.transpose(2, 0, 1, 3).reshape(row_count, q_heads, HD)
+    d_value = d_value_sum.astype(BF16).reshape(row_count, kv_heads * HD)
+    d_query_scaled = d_query_rot * cos_heads + rotate_back(d_query_rot * sin_heads)
+    d_key_scaled = d_key_rot * cos_heads + rotate_back(d_key_rot * sin_heads)
+    query_gain_part = jnp.sum(d_query_scaled * query_unit, axis=(0, 1))
+    key_gain_part = jnp.sum(d_key_scaled * key_unit, axis=(0, 1))
+    d_query = (
+        norm_back(d_query_scaled, query_unit, query_inv, query_gain)
+        .astype(BF16)
+        .reshape(row_count, q_heads * HD)
+    )
+    d_key = (
+        norm_back(d_key_scaled, key_unit, key_inv, key_gain)
+        .astype(BF16)
+        .reshape(row_count, kv_heads * HD)
+    )
+    features_one = feature_side(normed_one)
+    columns_one = jnp.concatenate(
+        [both_blocks(d_query), both_blocks(d_key), both_blocks(d_value)], axis=1
+    )
+    columns_one = jnp.concatenate([columns_one, to_pair(columns_one)], axis=0)
+    share_qkv, other_qkv_share = weight_share(features_one, columns_one)
+    d_normed_one = over_tensor(
+        mul_t(d_query, w_query) + mul_t(d_key, w_key) + mul_t(d_value, w_value)
+    )
+    grad_attn_gain = jnp.sum(d_normed_one * unit_one, axis=0)
+    d_input = from_local(
+        (d_resid + norm_back(d_normed_one, unit_one, inv_one, attn_gain)).astype(BF16)
+    )
+    gains = lax.psum(
+        jnp.concatenate(
+            [
+                from_local(0.5 * grad_attn_gain),
+                from_local(0.5 * grad_mlp_gain),
+                query_gain_part,
+                key_gain_part,
+            ]
+        ),
+        ("dp", "ctx", "tensor"),
+    )
+    owner = lax.axis_index("dp")
+
+    def owned_gain(start, size):
+        part = size // dp_size
+        return lax.dynamic_slice_in_dim(gains, start + owner * part, part)
+
+    def qkv_piece(low, high):
+        return whole(share_qkv[:, low:high], other_qkv_share[:, low:high])
+
+    return (
+        output[None],
+        d_input[None],
+        owned_gain(0, width),
+        qkv_piece(0, cut_q),
+        qkv_piece(cut_q, cut_k),
+        qkv_piece(cut_k, share_qkv.shape[1]),
+        owned_gain(2 * width, HD),
+        owned_gain(2 * width + HD, HD),
+        whole(*share_out).T,
+        owned_gain(width, width),
+        whole(*share_gate),
+        whole(*share_up),
+        whole(*share_down).T,
+    )
+
+
 def solution(mesh):
+    sizes = dict(mesh.shape)
+    body = per_device
+    if sizes["ctx"] == 2 and sizes["tensor"] == 2 and sizes["dp"] % 2 == 0:
+        body = functools.partial(paired_device, sizes["dp"])
     return jax.shard_map(
-        per_device,
+        body,
         mesh=mesh,
         in_specs=(
             P("dp", "ctx", None),

time: 1310 us -> 543 us (0.41)
  waiting for transfers between devices: 1130 us -> 217 us
  blocking collectives: 43.1 us -> 126 us
  starting transfers between devices: 1.16 us -> 41.3 us
  local copies, waits for them, and re-layouts: 32.6 us -> 51.1 us
    reduce_scatter x8 -> x5, waiting for transfers between devices: 675 us -> 0.05 us  [weight_share(): lax.psum_scatter(part, 'dp', axis_index_groups=line_groups, scatter_dimen...]
    all_gather x7 -> x1, waiting for transfers between devices: 331 us -> 0.02 us  [gather_line(): lax.all_gather(shard, 'dp', axis_index_groups=line_groups, axis=0, tiled=...]
    ppermute x0 -> x46, waiting for transfers between devices: none -> 217 us  [tree_exchange(): lax.ppermute(value, axis_name, [(i, i ^ 1) for i in range(axis_size)])]
    psum x4 -> x0, waiting for transfers between devices: 124 us -> none  [the longest x1 72.5 us: per_device(): lax.psum((share_a, share_q, share_k, share_v, share_qg, share_kg, share_o...]
    all_gather x2 -> x4, blocking collectives: 12.9 us -> 83.4 us  [gather_line(): lax.all_gather(shard, 'dp', axis_index_groups=line_groups, axis=0, tiled=...]
    ppermute x0 -> x46, starting transfers between devices: none -> 40.8 us  [tree_exchange(): lax.ppermute(value, axis_name, [(i, i ^ 1) for i in range(axis_size)])]
    psum x2 -> x1, blocking collectives: 8.08 us -> 42.3 us  [paired_device(): lax.psum(jnp.concatenate([from_local(0.5 * grad_attn_gain), from_local(0....]
    unnamed x1 -> x0, blocking collectives: 22.1 us -> none
  transfers between devices with their start and end apart: 19 -> 52, of which waited for: 19 -> 29; matrix products, arithmetic and copies ran while one was open for 5% -> 21% of each run, Pallas kernels for 0% -> 0%
where the time goes in v1:
time: 543 us; the launch traced here: 535 us
  waiting for transfers between devices  217 us (40%)
  blocking collectives  126 us (23%)
  local copies, waits for them, and re-layouts  51.1 us (9%)
  matrix products  50.9 us (9%)
  starting transfers between devices  41.3 us (8%)
  other arithmetic  32.7 us (6%)
  between operations  16.2 us (3%)
    ppermute x46, waiting for transfers between devices, tree_exchange(): lax.ppermute(value, axis_name, [(i, i ^ 1) for i in range(axis_size)])  217 us
    all_gather x4, blocking collectives, gather_line(): lax.all_gather(shard, 'dp', axis_index_groups=line_groups, axis=0, tiled=...  83.4 us
    psum x1, blocking collectives, paired_device(): lax.psum(jnp.concatenate([from_local(0.5 * grad_attn_gain), from_local(0....  42.3 us
    ppermute x46, starting transfers between devices, tree_exchange(): lax.ppermute(value, axis_name, [(i, i ^ 1) for i in range(axis_size)])  40.8 us
    dot_general x7, matrix products, mul_t(): return jnp.einsum('tf,df->td', value, weight, preferred_element_type=F32)  15.9 us
    unnamed x185, local copies, waits for them, and re-layouts  15.4 us
    dot_general x5, matrix products, weight_share(): jnp.einsum('td,tf->df', features, columns, preferred_element_type=F32)  12.2 us
  transfers between devices with their start and end apart: 52, of which 29 were waited for; matrix products, arithmetic and copies ran while one was open for 21% of the time, Pallas kernels for 0%

profile of v1, /device:TPU:0, one launch (start us, length us, event | category | flops | bytes accessed | tf_op | source)
XLA Modules:
  0.0 534.9 jit_solution(17440692406372687365)
XLA Ops:
  8.2 17.1 %all_gather.16 = bf16[512,512]{0,1:T(8,128)(2,1)} all-gather(bf16[128,512]{0,1:T(8,128)(2,1)S(1)} %dynamic-slice_bitcast_fusion.1), channel_id=1, replica_groups={{0,8,16,24},{4,12,20,28},{1,9,17,25},{5,13,21,29},{2,10,18,26},{6,14,22..., dimensions={0}, use_global_device_ids=true | all-gather | bytes 655360 | tf_op jit(solution)/shard_map/all_gather | solution.py:338
  31.0 26.9 %all_gather.19 = bf16[512,768]{0,1:T(8,128)(2,1)} all-gather(bf16[128,768]{0,1:T(8,128)(2,1)S(1)} %dynamic-slice_bitcast_fusion), channel_id=1, replica_groups={{0,8,16,24},{4,12,20,28},{1,9,17,25},{5,13,21,29},{2,10,18,26},{6,14,22..., dimensions={0}, use_global_device_ids=true | all-gather | bytes 983040 | tf_op jit(solution)/shard_map/all_gather | solution.py:338
  58.0 23.1 %all_gather.18 = bf16[512,768]{1,0:T(8,128)(2,1)} all-gather(bf16[128,768]{1,0:T(8,128)(2,1)S(1)} %constant_dynamic-slice_fusion), channel_id=1, replica_groups={{0,8,16,24},{4,12,20,28},{1,9,17,25},{5,13,21,29},{2,10,18,26},{6,14,22..., dimensions={0}, use_global_device_ids=true | all-gather | bytes 983040 | tf_op jit(solution)/shard_map/all_gather | solution.py:338
  88.4 26.6 %collective-permute-done = bf16[512,1024]{1,0:T(8,128)(2,1)} collective-permute-done((bf16[512,1024]{1,0:T(8,128)(2,1)}, bf16[512,1024]{1,0:T(8,128)(2,1)}, u32[]{:S(2)}, u32[]{:S(2)}) %collective-permute-start) | collective-permute-done | bytes 1048608 | tf_op jit(solution)/shard_map/ppermute | solution.py:278
  122.1 16.3 %all_gather.17 = bf16[512,768]{1,0:T(8,128)(2,1)} all-gather(bf16[128,768]{1,0:T(8,128)(2,1)S(1)} %constant_dynamic-slice_fusion.1), channel_id=1, replica_groups={{0,8,16,24},{4,12,20,28},{1,9,17,25},{5,13,21,29},{2,10,18,26},{6,14,22..., dimensions={0}, use_global_device_ids=true | all-gather | bytes 983040 | tf_op jit(solution)/shard_map/all_gather | solution.py:338
  141.3 13.3 %collective-permute-done.1 = bf16[1024,1024]{1,0:T(8,128)(2,1)S(1)} collective-permute-done((bf16[1024,1024]{1,0:T(8,128)(2,1)S(1)}, bf16[1024,1024]{1,0:T(8,128)(2,1)S(1)}, u32[]{:S(2)}, u32[]{:S(2)}) %collective-permute-start.1) | collective-permute-done | bytes 2097184 | tf_op jit(solution)/shard_map/ppermute | solution.py:278
  158.6 4.0 copy.50
  175.3 5.4 %collective-permute-done.2 = bf16[192,4,128]{2,0,1:T(8,128)(2,1)S(1)} collective-permute-done((bf16[192,4,128]{2,0,1:T(8,128)(2,1)S(1)}, bf16[192,4,128]{2,0,1:T(8,128)(2,1)S(1)}, u32[]{:S(2)}, u32[]{:S(2)}) %collective-permute-start.2) | collective-permute-done | bytes 196640 | tf_op jit(solution)/shard_map/ppermute | solution.py:278
  183.5 5.0 collective-permute-done.3
  193.7 4.2 collective-permute-done.6
  206.9 3.0 fusion.74
  211.8 15.3 %collective-permute-done.12 = bf16[1024,768]{1,0:T(8,128)(2,1)} collective-permute-done((bf16[1024,768]{1,0:T(8,128)(2,1)}, bf16[1024,768]{1,0:T(8,128)(2,1)}, u32[]{:S(2)}, u32[]{:S(2)}) %collective-permute-start.12) | collective-permute-done | bytes 1572896 | tf_op jit(solution)/shard_map/ppermute | solution.py:278
  229.2 10.7 %collective-permute-done.10 = bf16[512,768]{1,0:T(8,128)(2,1)S(1)} collective-permute-done((bf16[512,768]{1,0:T(8,128)(2,1)}, bf16[512,768]{1,0:T(8,128)(2,1)S(1)}, u32[]{:S(2)}, u32[]{:S(2)}) %collective-permute-start.10) | collective-permute-done | bytes 786464 | tf_op jit(solution)/shard_map/ppermute | solution.py:278
  242.7 3.2 fusion.6
  257.2 13.5 %collective-permute-done.30 = bf16[192,512]{1,0:T(8,128)(2,1)S(1)} collective-permute-done((bf16[192,512]{1,0:T(8,128)(2,1)S(1)}, bf16[192,512]{1,0:T(8,128)(2,1)S(1)}, u32[]{:S(2)}, u32[]{:S(2)}) %collective-permute-start.30) | collective-permute-done | bytes 196640 | tf_op jit(solution)/shard_map/ppermute | solution.py:278
  272.9 9.8 %collective-permute-done.31 = bf16[384,512]{1,0:T(8,128)(2,1)S(1)} collective-permute-done((bf16[384,512]{1,0:T(8,128)(2,1)S(1)}, bf16[384,512]{1,0:T(8,128)(2,1)S(1)}, u32[]{:S(2)}, u32[]{:S(2)}) %collective-permute-start.31) | collective-permute-done | bytes 393248 | tf_op jit(solution)/shard_map/ppermute | solution.py:278
  282.8 7.0 %collective-permute-done.29 = bf16[384,512]{1,0:T(8,128)(2,1)S(1)} collective-permute-done((bf16[384,512]{1,0:T(8,128)(2,1)S(1)}, bf16[384,512]{1,0:T(8,128)(2,1)S(1)}, u32[]{:S(2)}, u32[]{:S(2)}) %collective-permute-start.29) | collective-permute-done | bytes 393248 | tf_op jit(solution)/shard_map/ppermute | solution.py:278
  294.9 7.9 %collective-permute-done.35 = bf16[192,768]{1,0:T(8,128)(2,1)S(1)} collective-permute-done((bf16[192,768]{1,0:T(8,128)(2,1)S(1)}, bf16[192,768]{1,0:T(8,128)(2,1)S(1)}, u32[]{:S(2)}, u32[]{:S(2)}) %collective-permute-start.35) | collective-permute-done | bytes 294944 | tf_op jit(solution)/shard_map/ppermute | solution.py:278
  303.1 5.7 %collective-permute-done.33 = bf16[192,1024]{1,0:T(8,128)(2,1)S(1)} collective-permute-done((bf16[192,1024]{1,0:T(8,128)(2,1)}, bf16[192,1024]{1,0:T(8,128)(2,1)S(1)}, u32[]{:S(2)}, u32[]{:S(2)}) %collective-permute-start.33) | collective-permute-done | bytes 393248 | tf_op jit(solution)/shard_map/ppermute | solution.py:278
  309.6 12.5 %collective-permute-done.34 = bf16[384,512]{1,0:T(8,128)(2,1)S(1)} collective-permute-done((bf16[384,512]{1,0:T(8,128)(2,1)S(1)}, bf16[384,512]{1,0:T(8,128)(2,1)S(1)}, u32[]{:S(2)}, u32[]{:S(2)}) %collective-permute-start.34) | collective-permute-done | bytes 393248 | tf_op jit(solution)/shard_map/ppermute | solution.py:278
  328.2 8.8 %collective-permute-done.41 = bf16[192,1024]{1,0:T(8,128)(2,1)S(1)} collective-permute-done((bf16[192,1024]{1,0:T(8,128)(2,1)S(1)}, bf16[192,1024]{1,0:T(8,128)(2,1)S(1)}, u32[]{:S(2)}, u32[]{:S(2)}) %collective-permute-start.41) | collective-permute-done | bytes 393248 | tf_op jit(solution)/shard_map/ppermute | solution.py:278
  337.4 4.1 collective-permute-done.43
  346.4 17.2 %collective-permute-done.42 = bf16[384,512]{1,0:T(8,128)(2,1)S(1)} collective-permute-done((bf16[384,512]{1,0:T(8,128)(2,1)S(1)}, bf16[384,512]{1,0:T(8,128)(2,1)S(1)}, u32[]{:S(2)}, u32[]{:S(2)}) %collective-permute-start.42) | collective-permute-done | bytes 393248 | tf_op jit(solution)/shard_map/ppermute | solution.py:278
  365.6 3.1 convolution_convert_fusion
  386.5 3.1 fusion.36
  412.6 11.3 %collective-permute-done.22 = bf16[384,512]{1,0:T(8,128)(2,1)S(1)} collective-permute-done((bf16[384,512]{1,0:T(8,128)(2,1)S(1)}, bf16[384,512]{1,0:T(8,128)(2,1)S(1)}, u32[]{:S(2)}, u32[]{:S(2)}) %collective-permute-start.22) | collective-permute-done | bytes 393248 | tf_op jit(solution)/shard_map/ppermute | solution.py:278
  423.9 3.3 fusion.8
  438.0 42.3 %psum.7 = f32[2304]{0:T(1024)S(1)} all-reduce(f32[2304]{0:T(1024)S(1)} %pad_maximum_fusion.26), channel_id=1, replica_groups=mesh['dp'=8,'ctx'=2,'tensor'=2] {'dp','ctx','tensor'}, use_global_device_ids=true, to_apply=%region_15.16 | all-reduce | flops 2304 | bytes 18432 | tf_op jit(solution)/shard_map/psum | solution.py:532
  493.2 5.3 collective-permute-done.37
  501.6 5.4 %collective-permute-done.45 = f32[128,768]{1,0:T(8,128)S(1)} collective-permute-done((f32[128,768]{1,0:T(8,128)}, f32[128,768]{1,0:T(8,128)S(1)}, u32[]{:S(2)}, u32[]{:S(2)}) %collective-permute-start.45) | collective-permute-done | bytes 393248 | tf_op jit(solution)/shard_map/ppermute | solution.py:278
  508.2 7.2 %collective-permute-done.40 = f32[128,768]{1,0:T(8,128)S(1)} collective-permute-done((f32[128,768]{1,0:T(8,128)}, f32[128,768]{1,0:T(8,128)S(1)}, u32[]{:S(2)}, u32[]{:S(2)}) %collective-permute-start.40) | collective-permute-done | bytes 393248 | tf_op jit(solution)/shard_map/ppermute | solution.py:278
  516.4 8.8 %collective-permute-done.27 = f32[128,1024]{1,0:T(8,128)S(1)} collective-permute-done((f32[128,1024]{1,0:T(8,128)}, f32[128,1024]{1,0:T(8,128)S(1)}, u32[]{:S(2)}, u32[]{:S(2)}) %collective-permute-start.27) | collective-permute-done | bytes 524320 | tf_op jit(solution)/shard_map/ppermute | solution.py:278
  (427 shorter events, 168.2 us)
Async XLA Ops:
  7.2 76.9 %all-gather.2.cloned.1.call-start = ((), (), s32[]{:S(2)}) async-start(), calls=%async_computation.5 | async-start | bytes 1310720 | tf_op jit(solution)/shard_map/all_gather | solution.py:338
  25.3 156.3 %collective-permute-start.5 = (bf16[512,512]{0,1:T(8,128)(2,1)}, bf16[512,512]{0,1:T(8,128)(2,1)}, u32[]{:S(2)}, u32[]{:S(2)}) collective-permute-start(bf16[512,512]{0,1:T(8,128)(2,1)} %all_gather.16), channel_id=1, source_target_pairs={{0,2},{2,0},{1,3},{3,1},{4,6},{6,4},{5,7},{7,5},{8,10},{10,8},{9,1... | collective-permute-start | bytes 1572872 | tf_op jit(solution)/shard_map/ppermute | solution.py:278
  26.8 164.5 %collective-permute-start.4 = (bf16[512,512]{0,1:T(8,128)(2,1)}, bf16[512,512]{0,1:T(8,128)(2,1)}, u32[]{:S(2)}, u32[]{:S(2)}) collective-permute-start(bf16[512,512]{0,1:T(8,128)(2,1)} %all_gather.16), channel_id=1, source_target_pairs={{0,4},{4,0},{8,12},{12,8},{16,20},{20,16},{24,28},{28,24},{1,5},{5... | collective-permute-start | bytes 1572872 | tf_op jit(solution)/shard_map/ppermute | solution.py:278
  30.9 449.5 %reduce-scatter.8.cloned.1.call-start = ((), (), s32[]{:S(2)}) async-start(), calls=%async_computation.7 | async-start | bytes 1310720 | tf_op jit(solution)/shard_map/reduce_scatter | solution.py:384
  57.9 133.8 %collective-permute-start.14 = (bf16[512,768]{0,1:T(8,128)(2,1)}, bf16[512,768]{0,1:T(8,128)(2,1)}, u32[]{:S(2)}, u32[]{:S(2)}) collective-permute-start(bf16[512,768]{0,1:T(8,128)(2,1)} %all_gather.19), channel_id=1, source_target_pairs={{0,2},{2,0},{1,3},{3,1},{4,6},{6,4},{5,7},{7,5},{8,10},{10,8},{9,1... | collective-permute-start | bytes 2359304 | tf_op jit(solution)/shard_map/ppermute | solution.py:278
  81.0 57.4 %collective-permute-start.11 = (bf16[512,768]{1,0:T(8,128)(2,1)}, bf16[512,768]{1,0:T(8,128)(2,1)}, u32[]{:S(2)}, u32[]{:S(2)}) collective-permute-start(bf16[512,768]{1,0:T(8,128)(2,1)} %all_gather.18), channel_id=1, source_target_pairs={{0,4},{4,0},{8,12},{12,8},{16,20},{20,16},{24,28},{28,24},{1,5},{5... | collective-permute-start | bytes 2359304 | tf_op jit(solution)/shard_map/ppermute | solution.py:278
  84.1 30.8 %collective-permute-start = (bf16[512,1024]{1,0:T(8,128)(2,1)}, bf16[512,1024]{1,0:T(8,128)(2,1)}, u32[]{:S(2)}, u32[]{:S(2)}) collective-permute-start(bf16[512,1024]{1,0:T(8,128)(2,1)} %all-gather.2.cloned.1.call-done), channel_id=1, source_target_pairs={{0,4},{4,0},{8,12},{12,8},{16,20},{20,16},{24,28},{28,24},{1,5},{5... | collective-permute-start | bytes 3145736 | tf_op jit(solution)/shard_map/ppermute | solution.py:278
  116.2 38.4 %collective-permute-start.1 = (bf16[1024,1024]{1,0:T(8,128)(2,1)S(1)}, bf16[1024,1024]{1,0:T(8,128)(2,1)S(1)}, u32[]{:S(2)}, u32[]{:S(2)}) collective-permute-start(bf16[1024,1024]{1,0:T(8,128)(2,1)S(1)} %constant_dynamic-update-slice_fusion), channel_id=1, source_target_pairs={{0,2},{2,0},{1,3},{3,1},{4,6},{6,4},{5,7},{7,5},{8,10},{10,8},{9,1... | collective-permute-start | bytes 6291464 | tf_op jit(solution)/shard_map/ppermute | solution.py:278
  138.4 64.0 %collective-permute-start.13 = (bf16[512,768]{0,1:T(8,128)(2,1)}, bf16[512,768]{0,1:T(8,128)(2,1)}, u32[]{:S(2)}, u32[]{:S(2)}) collective-permute-start(bf16[512,768]{0,1:T(8,128)(2,1)} %all_gather.19), channel_id=1, source_target_pairs={{0,4},{4,0},{8,12},{12,8},{16,20},{20,16},{24,28},{28,24},{1,5},{5... | collective-permute-start | bytes 2359304 | tf_op jit(solution)/shard_map/ppermute | solution.py:278
  181.7 23.7 %collective-permute-start.9 = (bf16[512,768]{1,0:T(8,128)(2,1)}, bf16[512,768]{1,0:T(8,128)(2,1)}, u32[]{:S(2)}, u32[]{:S(2)}) collective-permute-start(bf16[512,768]{1,0:T(8,128)(2,1)} %all_gather.17), channel_id=1, source_target_pairs={{0,2},{2,0},{1,3},{3,1},{4,6},{6,4},{5,7},{7,5},{8,10},{10,8},{9,1... | collective-permute-start | bytes 2359304 | tf_op jit(solution)/shard_map/ppermute | solution.py:278
  191.3 35.7 %collective-permute-start.12 = (bf16[1024,768]{1,0:T(8,128)(2,1)}, bf16[1024,768]{1,0:T(8,128)(2,1)}, u32[]{:S(2)}, u32[]{:S(2)}) collective-permute-start(bf16[1024,768]{1,0:T(8,128)(2,1)} %copy-done.42), channel_id=1, source_target_pairs={{0,2},{2,0},{1,3},{3,1},{4,6},{6,4},{5,7},{7,5},{8,10},{10,8},{9,1... | collective-permute-start | bytes 4718600 | tf_op jit(solution)/shard_map/ppermute | solution.py:278
  202.4 26.8 %collective-permute-start.8 = (bf16[512,768]{1,0:T(8,128)(2,1)}, bf16[512,768]{1,0:T(8,128)(2,1)S(1)}, u32[]{:S(2)}, u32[]{:S(2)}) collective-permute-start(bf16[512,768]{1,0:T(8,128)(2,1)} %all_gather.17), channel_id=1, source_target_pairs={{0,4},{4,0},{8,12},{12,8},{16,20},{20,16},{24,28},{28,24},{1,5},{5... | collective-permute-start | bytes 2359304 | tf_op jit(solution)/shard_map/ppermute | solution.py:278
  205.4 34.6 %collective-permute-start.10 = (bf16[512,768]{1,0:T(8,128)(2,1)}, bf16[512,768]{1,0:T(8,128)(2,1)S(1)}, u32[]{:S(2)}, u32[]{:S(2)}) collective-permute-start(bf16[512,768]{1,0:T(8,128)(2,1)} %collective-permute-done.9), channel_id=1, source_target_pairs={{0,4},{4,0},{8,12},{12,8},{16,20},{20,16},{24,28},{28,24},{1,5},{5... | collective-permute-start | bytes 2359304 | tf_op jit(solution)/shard_map/ppermute | solution.py:278
  255.1 15.7 %collective-permute-start.28 = (bf16[192,1024]{1,0:T(8,128)(2,1)S(1)}, bf16[192,1024]{1,0:T(8,128)(2,1)S(1)}, u32[]{:S(2)}, u32[]{:S(2)}) collective-permute-start(bf16[192,1024]{1,0:T(8,128)(2,1)S(1)} %get-tuple-element.48), channel_id=1, source_target_pairs={{0,2},{2,0},{1,3},{3,1},{4,6},{6,4},{5,7},{7,5},{8,10},{10,8},{9,1... | collective-permute-start | bytes 1179656 | tf_op jit(solution)/shard_map/ppermute | solution.py:278
  270.9 18.9 %collective-permute-start.29 = (bf16[384,512]{1,0:T(8,128)(2,1)S(1)}, bf16[384,512]{1,0:T(8,128)(2,1)S(1)}, u32[]{:S(2)}, u32[]{:S(2)}) collective-permute-start(bf16[384,512]{1,0:T(8,128)(2,1)S(1)} %get-tuple-element.64), channel_id=1, source_target_pairs={{0,4},{4,0},{8,12},{12,8},{16,20},{20,16},{24,28},{28,24},{1,5},{5... | collective-permute-start | bytes 1179656 | tf_op jit(solution)/shard_map/ppermute | solution.py:278
  291.6 191.2 %reduce-scatter.10.cloned.1.call-start = ((), (), s32[]{:S(2)}) async-start(), calls=%async_computation.8 | async-start | bytes 1966080 | tf_op jit(solution)/shard_map/reduce_scatter | solution.py:384
  293.1 15.7 %collective-permute-start.33 = (bf16[192,1024]{1,0:T(8,128)(2,1)}, bf16[192,1024]{1,0:T(8,128)(2,1)S(1)}, u32[]{:S(2)}, u32[]{:S(2)}) collective-permute-start(bf16[192,1024]{1,0:T(8,128)(2,1)} %copy-done.25), channel_id=1, source_target_pairs={{0,2},{2,0},{1,3},{3,1},{4,6},{6,4},{5,7},{7,5},{8,10},{10,8},{9,1... | collective-permute-start | bytes 1179656 | tf_op jit(solution)/shard_map/ppermute | solution.py:278
  302.8 19.3 %collective-permute-start.36 = (bf16[384,768]{1,0:T(8,128)(2,1)S(1)}, bf16[384,768]{1,0:T(8,128)(2,1)S(1)}, u32[]{:S(2)}, u32[]{:S(2)}) collective-permute-start(bf16[384,768]{1,0:T(8,128)(2,1)S(1)} %pad_maximum_fusion.15), channel_id=1, source_target_pairs={{0,4},{4,0},{8,12},{12,8},{16,20},{20,16},{24,28},{28,24},{1,5},{5... | collective-permute-start | bytes 1769480 | tf_op jit(solution)/shard_map/ppermute | solution.py:278
  324.9 158.9 %reduce-scatter.14.cloned.1.call-start = ((), (), s32[]{:S(2)}) async-start(), calls=%async_computation.10 | async-start | bytes 1966080 | tf_op jit(solution)/shard_map/reduce_scatter | solution.py:384
  341.5 22.1 %collective-permute-start.44 = (bf16[384,768]{1,0:T(8,128)(2,1)S(1)}, bf16[384,768]{1,0:T(8,128)(2,1)S(1)}, u32[]{:S(2)}, u32[]{:S(2)}) collective-permute-start(bf16[384,768]{1,0:T(8,128)(2,1)S(1)} %pad_maximum_fusion.17), channel_id=1, source_target_pairs={{0,4},{4,0},{8,12},{12,8},{16,20},{20,16},{24,28},{28,24},{1,5},{5... | collective-permute-start | bytes 1769480 | tf_op jit(solution)/shard_map/ppermute | solution.py:278
  342.5 21.1 %collective-permute-start.42 = (bf16[384,512]{1,0:T(8,128)(2,1)S(1)}, bf16[384,512]{1,0:T(8,128)(2,1)S(1)}, u32[]{:S(2)}, u32[]{:S(2)}) collective-permute-start(bf16[384,512]{1,0:T(8,128)(2,1)S(1)} %get-tuple-element.60), channel_id=1, source_target_pairs={{0,4},{4,0},{8,12},{12,8},{16,20},{20,16},{24,28},{28,24},{1,5},{5... | collective-permute-start | bytes 1179656 | tf_op jit(solution)/shard_map/ppermute | solution.py:278
  345.5 41.0 %collective-permute-start.39 = (bf16[384,768]{1,0:T(8,128)(2,1)}, bf16[384,768]{1,0:T(8,128)(2,1)}, u32[]{:S(2)}, u32[]{:S(2)}) collective-permute-start(bf16[384,768]{1,0:T(8,128)(2,1)} %pad_maximum_fusion.16), channel_id=1, source_target_pairs={{0,4},{4,0},{8,12},{12,8},{16,20},{20,16},{24,28},{28,24},{1,5},{5... | collective-permute-start | bytes 1769480 | tf_op jit(solution)/shard_map/ppermute | solution.py:278
  365.5 125.7 %reduce-scatter.12.cloned.1.call-start = ((), (), s32[]{:S(2)}) async-start(), calls=%async_computation.9 | async-start | bytes 1966080 | tf_op jit(solution)/shard_map/reduce_scatter | solution.py:384
  374.4 15.6 %collective-permute-start.19 = (f32[192,4,128]{0,2,1:T(8,128)}, f32[192,4,128]{0,2,1:T(8,128)}, u32[]{:S(2)}, u32[]{:S(2)}) collective-permute-start(f32[192,4,128]{0,2,1:T(8,128)} %slice.337), channel_id=1, source_target_pairs={{0,2},{2,0},{1,3},{3,1},{4,6},{6,4},{5,7},{7,5},{8,10},{10,8},{9,1... | collective-permute-start | bytes 1179656 | tf_op jit(solution)/shard_map/ppermute | solution.py:278
  380.5 16.3 %collective-permute-start.18 = (f32[192,4,128]{2,0,1:T(8,128)}, f32[192,4,128]{2,0,1:T(8,128)}, u32[]{:S(2)}, u32[]{:S(2)}) collective-permute-start(f32[192,4,128]{2,0,1:T(8,128)} %slice.331), channel_id=1, source_target_pairs={{0,2},{2,0},{1,3},{3,1},{4,6},{6,4},{5,7},{7,5},{8,10},{10,8},{9,1... | collective-permute-start | bytes 1179656 | tf_op jit(solution)/shard_map/ppermute | solution.py:278
  386.0 18.5 %collective-permute-start.23 = (bf16[192,512]{1,0:T(8,128)(2,1)}, bf16[192,512]{1,0:T(8,128)(2,1)}, u32[]{:S(2)}, u32[]{:S(2)}) collective-permute-start(bf16[192,512]{1,0:T(8,128)(2,1)} %get-tuple-element.87), channel_id=1, source_target_pairs={{0,2},{2,0},{1,3},{3,1},{4,6},{6,4},{5,7},{7,5},{8,10},{10,8},{9,1... | collective-permute-start | bytes 589832 | tf_op jit(solution)/shard_map/ppermute | solution.py:278
  389.7 109.9 %reduce-scatter.6.cloned.1.call-start = ((), (), s32[]{:S(2)}) async-start(), calls=%async_computation.6 | async-start | bytes 2621440 | tf_op jit(solution)/shard_map/reduce_scatter | solution.py:384
  407.6 16.3 %collective-permute-start.26 = (bf16[384,1024]{1,0:T(8,128)(2,1)S(1)}, bf16[384,1024]{1,0:T(8,128)(2,1)S(1)}, u32[]{:S(2)}, u32[]{:S(2)}) collective-permute-start(bf16[384,1024]{1,0:T(8,128)(2,1)S(1)} %maximum_maximum_fusion.3), channel_id=1, source_target_pairs={{0,4},{4,0},{8,12},{12,8},{16,20},{20,16},{24,28},{28,24},{1,5},{5... | collective-permute-start | bytes 2359304 | tf_op jit(solution)/shard_map/ppermute | solution.py:278
  482.8 15.8 %collective-permute-start.37 = (f32[128,768]{1,0:T(8,128)}, f32[128,768]{1,0:T(8,128)S(1)}, u32[]{:S(2)}, u32[]{:S(2)}) collective-permute-start(f32[128,768]{1,0:T(8,128)} %reduce-scatter.10.cloned.1.call-done), channel_id=1, source_target_pairs={{0,2},{2,0},{1,3},{3,1},{4,6},{6,4},{5,7},{7,5},{8,10},{10,8},{9,1... | collective-permute-start | bytes 1179656 | tf_op jit(solution)/shard_map/ppermute | solution.py:278
  483.8 23.2 %collective-permute-start.45 = (f32[128,768]{1,0:T(8,128)}, f32[128,768]{1,0:T(8,128)S(1)}, u32[]{:S(2)}, u32[]{:S(2)}) collective-permute-start(f32[128,768]{1,0:T(8,128)} %reduce-scatter.14.cloned.1.call-done), channel_id=1, source_target_pairs={{0,2},{2,0},{1,3},{3,1},{4,6},{6,4},{5,7},{7,5},{8,10},{10,8},{9,1... | collective-permute-start | bytes 1179656 | tf_op jit(solution)/shard_map/ppermute | solution.py:278
  491.2 24.2 %collective-permute-start.40 = (f32[128,768]{1,0:T(8,128)}, f32[128,768]{1,0:T(8,128)S(1)}, u32[]{:S(2)}, u32[]{:S(2)}) collective-permute-start(f32[128,768]{1,0:T(8,128)} %reduce-scatter.12.cloned.1.call-done), channel_id=1, source_target_pairs={{0,2},{2,0},{1,3},{3,1},{4,6},{6,4},{5,7},{7,5},{8,10},{10,8},{9,1... | collective-permute-start | bytes 1179656 | tf_op jit(solution)/shard_map/ppermute | solution.py:278
  499.5 25.7 %collective-permute-start.27 = (f32[128,1024]{1,0:T(8,128)}, f32[128,1024]{1,0:T(8,128)S(1)}, u32[]{:S(2)}, u32[]{:S(2)}) collective-permute-start(f32[128,1024]{1,0:T(8,128)} %reduce-scatter.6.cloned.1.call-done), channel_id=1, source_target_pairs={{0,2},{2,0},{1,3},{3,1},{4,6},{6,4},{5,7},{7,5},{8,10},{10,8},{9,1... | collective-permute-start | bytes 1572872 | tf_op jit(solution)/shard_map/ppermute | solution.py:278
  (109 other events, 964.9 us)
Sparse Core Ops, SparseCore 0:
  31.0 37.6 all-gather.1
  291.7 24.6 reduce-scatter.7
  325.0 32.7 reduce-scatter.9
  365.7 32.9 reduce-scatter.13
  400.8 34.2 reduce-scatter.11
  437.3 43.5 reduce-scatter.5

commit v2 on v1

--- a/solution.py
+++ b/solution.py
@@ -339,45 +339,40 @@
             shard, "dp", axis_index_groups=line_groups, axis=0, tiled=True
         )
 
-    def spread_pair_first(part):
-        part = jnp.concatenate([part, to_pair(part)], axis=0)
-        return part, to_ctx(part)
-
-    def spread_ctx_first(part):
-        other = to_ctx(part)
-        return (
-            jnp.concatenate([part, to_pair(part)], axis=0),
-            jnp.concatenate([other, to_pair(other)], axis=0),
-        )
-
-    halves = [own_half(shard) for shard in (query_weight, key_weight, value_weight)]
-    cut_q = halves[0].shape[1]
-    cut_k = cut_q + halves[1].shape[1]
-    own_qkv, other_qkv = spread_pair_first(gather_line(jnp.concatenate(halves, axis=1)))
-
-    def both(low, high):
-        return jnp.concatenate([own_qkv[:, low:high], other_qkv[:, low:high]], axis=1)
-
-    w_query, w_key, w_value = both(0, cut_q), both(cut_q, cut_k), both(cut_k, own_qkv.shape[1])
-    w_out_t = jnp.concatenate(
-        spread_ctx_first(gather_line(own_half(output_weight.T))), axis=1
-    )
-    w_gate = jnp.concatenate(spread_ctx_first(gather_line(own_half(gate_weight))), axis=1)
-    w_up = jnp.concatenate(spread_pair_first(gather_line(own_half(up_weight))), axis=1)
-    w_down_t = jnp.concatenate(spread_ctx_first(gather_line(own_half(down_weight.T))), axis=1)
-
-    def both_blocks(value):
+    def to_diagonal(value):
+        steps = [(i, i ^ 3) for i in range(2 * dp_size)]
+        return lax.ppermute(value, ("dp", "ctx"), steps)
+
+    def gather(shards):
+        shards = [own_half(shard) for shard in shards]
+        part = gather_line(jnp.concatenate(shards, axis=1))
+        over_ctx, over_pair = to_ctx(part), to_pair(part)
+        middle = part.shape[1] // 2
+        diagonal = jnp.concatenate(
+            [to_ctx(over_pair[:, :middle]), to_pair(over_ctx[:, middle:])], axis=1
+        )
+        found, low = [], 0
+        for shard in shards:
+            high = low + shard.shape[1]
+            top = jnp.concatenate([part[:, low:high], over_ctx[:, low:high]], axis=1)
+            bottom = jnp.concatenate([over_pair[:, low:high], diagonal[:, low:high]], axis=1)
+            found.append(jnp.concatenate([top, bottom], axis=0))
+            low = high
+        return found
+
+    w_query, w_key, w_value = gather([query_weight, key_weight, value_weight])
+    w_out_t, w_gate = gather([output_weight.T, gate_weight])
+    w_up, w_down_t = gather([up_weight, down_weight.T])
+
+    def feature_side(value):
         half = value.shape[1] // 2
-        return jnp.concatenate([value[:, :half], to_ctx(value[:, half:])], axis=0)
-
-    def feature_side(value):
-        value = jnp.concatenate([value, to_ctx(value)], axis=0)
-        half = value.shape[1] // 2
-        return jnp.concatenate([value[:, :half], to_pair(value[:, half:])], axis=0)
-
-    def column_side(value):
-        value = both_blocks(value)
-        return jnp.concatenate([value, to_pair(value)], axis=0)
+        own, far = value[:, :half], value[:, half:]
+        return jnp.concatenate([own, to_ctx(own), to_pair(far), to_diagonal(far)], axis=0)
+
+    def column_side(values):
+        own = jnp.concatenate([value[:, : value.shape[1] // 2] for value in values], axis=1)
+        far = jnp.concatenate([value[:, value.shape[1] // 2 :] for value in values], axis=1)
+        return jnp.concatenate([own, to_ctx(far), to_pair(own), to_diagonal(far)], axis=0)
 
     def weight_share(features, columns):
         part = jnp.einsum("td,tf->df", features, columns, preferred_element_type=F32)
@@ -463,6 +458,9 @@
     inv_two = rms_inverse(resid)
     unit_two = resid * inv_two
     normed_two = (unit_two * mlp_gain).astype(BF16)
+    features_down = feature_side(d_output)
+    features_two = feature_side(normed_two)
+    columns_out = column_side([attn])
     gate = jnp.dot(normed_two, w_gate, preferred_element_type=F32)
     up_proj = jnp.dot(normed_two, w_up, preferred_element_type=F32)
     sigma = jax.nn.sigmoid(gate)
@@ -470,18 +468,20 @@
     hidden = (silu_gate * up_proj).astype(BF16)
     output = from_local((resid + over_tensor(mul_t(hidden, w_down_t))).astype(BF16))
 
-    share_down = weight_share(feature_side(d_output), column_side(hidden))
+    features_down, hidden = lax.optimization_barrier((features_down, hidden))
+    share_down = weight_share(features_down, column_side([hidden]))
     d_hidden = jnp.dot(d_output, w_down_t, preferred_element_type=F32)
     d_gate = (d_hidden * up_proj * sigma * (1.0 + gate * (1.0 - sigma))).astype(BF16)
     d_up = (d_hidden * silu_gate).astype(BF16)
-    features_two = feature_side(normed_two)
-    share_gate = weight_share(features_two, column_side(d_gate))
-    share_up = weight_share(features_two, column_side(d_up))
+    features_two, columns_out, d_gate, d_up = lax.optimization_barrier(
+        (features_two, columns_out, d_gate, d_up)
+    )
+    share_mlp, other_mlp = weight_share(features_two, column_side([d_gate, d_up]))
     d_normed_two = over_tensor(mul_t(d_gate, w_gate) + mul_t(d_up, w_up))
     grad_mlp_gain = jnp.sum(d_normed_two * unit_two, axis=0)
     d_resid = d_output.astype(F32) + norm_back(d_normed_two, unit_two, inv_two, mlp_gain)
     d_resid_b = d_resid.astype(BF16)
-    share_out = weight_share(feature_side(d_resid_b), column_side(attn))
+    share_out = weight_share(feature_side(d_resid_b), columns_out)
     d_attn = jnp.dot(d_resid_b, w_out_t, preferred_element_type=F32).astype(BF16)
     delta = jnp.sum(
         d_attn.astype(F32).reshape(row_count, q_heads, HD)
@@ -517,10 +517,10 @@
         .reshape(row_count, kv_heads * HD)
     )
     features_one = feature_side(normed_one)
-    columns_one = jnp.concatenate(
-        [both_blocks(d_query), both_blocks(d_key), both_blocks(d_value)], axis=1
-    )
-    columns_one = jnp.concatenate([columns_one, to_pair(columns_one)], axis=0)
+    features_one, share_down, d_query, d_key, d_value = lax.optimization_barrier(
+        (features_one, share_down, d_query, d_key, d_value)
+    )
+    columns_one = column_side([d_query, d_key, d_value])
     share_qkv, other_qkv_share = weight_share(features_one, columns_one)
     d_normed_one = over_tensor(
         mul_t(d_query, w_query) + mul_t(d_key, w_key) + mul_t(d_value, w_value)
@@ -529,7 +529,7 @@
     d_input = from_local(
         (d_resid + norm_back(d_normed_one, unit_one, inv_one, attn_gain)).astype(BF16)
     )
-    gains = lax.psum(
+    gains = over_tensor(
         jnp.concatenate(
             [
                 from_local(0.5 * grad_attn_gain),
@@ -537,9 +537,16 @@
                 query_gain_part,
                 key_gain_part,
             ]
-        ),
-        ("dp", "ctx", "tensor"),
-    )
+        )
+    )
+    share_mlp, other_mlp, share_out, gains = lax.optimization_barrier(
+        (share_mlp, other_mlp, share_out, gains)
+    )
+    gains = gains + to_ctx(gains)
+    stride = 1
+    while stride < dp_size:
+        gains = gains + lax.ppermute(gains, "dp", [(i, i ^ stride) for i in range(dp_size)])
+        stride *= 2
     owner = lax.axis_index("dp")
 
     def owned_gain(start, size):
@@ -548,6 +555,10 @@
 
     def qkv_piece(low, high):
         return whole(share_qkv[:, low:high], other_qkv_share[:, low:high])
+
+    cut_q = query_weight.shape[1] // 2
+    cut_k = cut_q + key_weight.shape[1] // 2
+    cut_g = gate_weight.shape[1] // 2
 
     return (
         output[None],
@@ -560,8 +571,8 @@
         owned_gain(2 * width + HD, HD),
         whole(*share_out).T,
         owned_gain(width, width),
-        whole(*share_gate),
-        whole(*share_up),
+        whole(share_mlp[:, :cut_g], other_mlp[:, :cut_g]),
+        whole(share_mlp[:, cut_g:], other_mlp[:, cut_g:]),
         whole(*share_down).T,
     )
 
@@ -569,7 +580,7 @@
 def solution(mesh):
     sizes = dict(mesh.shape)
     body = per_device
-    if sizes["ctx"] == 2 and sizes["tensor"] == 2 and sizes["dp"] % 2 == 0:
+    if sizes["ctx"] == 2 and sizes["tensor"] == 2 and sizes["dp"] in (2, 4, 8, 16):
         body = functools.partial(paired_device, sizes["dp"])
     return jax.shard_map(
         body,

time: 543 us -> 495 us (0.912)
  blocking collectives: 126 us -> 0 us
  waiting for transfers between devices: 217 us -> 245 us
  other arithmetic: 32.7 us -> 51.1 us
  starting transfers between devices: 41.3 us -> 58.2 us
  local copies, waits for them, and re-layouts: 51.1 us -> 64.3 us
    all_gather x4 -> x0, blocking collectives: 83.4 us -> none  [gather_line(): lax.all_gather(shard, 'dp', axis_index_groups=line_groups, axis=0, tiled=...]
    all_gather x1 -> x3, waiting for transfers between devices: 0.02 us -> 70.2 us  [gather_line(): lax.all_gather(shard, 'dp', axis_index_groups=line_groups, axis=0, tiled=...]
    ppermute x46 -> x42, waiting for transfers between devices: 217 us -> 165 us  [tree_exchange(): lax.ppermute(value, axis_name, [(i, i ^ 1) for i in range(axis_size)])]
    psum x1 -> x0, blocking collectives: 42.3 us -> none  [paired_device(): lax.psum(jnp.concatenate([from_local(0.5 * grad_attn_gain), from_local(0....]
    slice x12 -> x32, local copies, waits for them, and re-layouts: 6.66 us -> 32.3 us  [the longest x9 15.6 us: gather(): top = jnp.concatenate([part[:, low:high], over_ctx[:, low:high]], axis=1)]
    concatenate x9 -> x12, other arithmetic: 4.13 us -> 20.5 us  [the longest x1 10.9 us: gather(): found.append(jnp.concatenate([top, bottom], axis=0))]
    ppermute x0 -> x11, starting transfers between devices: none -> 14.1 us  [the longest x8 13.5 us: to_diagonal(): return lax.ppermute(value, ('dp', 'ctx'), steps)]
    dot_general x1, matrix products: 3.02 us -> 12.6 us  [paired_device(): d_hidden = jnp.dot(d_output, w_down_t, preferred_element_type=F32)]
  transfers between devices with their start and end apart: 52 -> 60, of which waited for: 29 -> 28; matrix products, arithmetic and copies ran while one was open for 21% -> 32% of each run, Pallas kernels for 0% -> 0%
where the time goes in v2:
time: 495 us; the launch traced here: 487 us
  waiting for transfers between devices  245 us (49%)
  local copies, waits for them, and re-layouts  64.3 us (13%)
  starting transfers between devices  58.2 us (12%)
  matrix products  51.6 us (10%)
  other arithmetic  51.1 us (10%)
  between operations  16.7 us (3%)
    ppermute x42, waiting for transfers between devices, tree_exchange(): lax.ppermute(value, axis_name, [(i, i ^ 1) for i in range(axis_size)])  165 us
    all_gather x3, waiting for transfers between devices, gather_line(): lax.all_gather(shard, 'dp', axis_index_groups=line_groups, axis=0, tiled=...  70.2 us
    ppermute x42, starting transfers between devices, tree_exchange(): lax.ppermute(value, axis_name, [(i, i ^ 1) for i in range(axis_size)])  43.5 us
    slice x9, local copies, waits for them, and re-layouts, gather(): top = jnp.concatenate([part[:, low:high], over_ctx[:, low:high]], axis=1)  15.6 us
    ppermute x8, starting transfers between devices, to_diagonal(): return lax.ppermute(value, ('dp', 'ctx'), steps)  13.5 us
    dot_general x7, matrix products, mul_t(): return jnp.einsum('tf,df->td', value, weight, preferred_element_type=F32)  12.9 us
    dot_general x1, matrix products, paired_device(): d_hidden = jnp.dot(d_output, w_down_t, preferred_element_type=F32)  12.6 us
    concatenate x1, other arithmetic, gather(): found.append(jnp.concatenate([top, bottom], axis=0))  10.9 us
  transfers between devices with their start and end apart: 60, of which 28 were waited for; matrix products, arithmetic and copies ran while one was open for 32% of the time, Pallas kernels for 0%

profile of v2, /device:TPU:0, one launch (start us, length us, event | category | flops | bytes accessed | tf_op | source)
XLA Modules:
  0.0 487.2 jit_solution(2048732008326785946)
XLA Ops:
  14.3 3.0 collective-permute-start.27
  25.5 15.4 %all-gather.4.cloned.1.call-done = bf16[512,1024]{1,0:T(8,128)(2,1)} async-done(((bf16[128,1024]{1,0:T(8,128)(2,1)}), bf16[512,1024]{1,0:T(8,128)(2,1)}) %all-gather.4.cloned.1.call-update) | async-done | bytes 1048592 | tf_op jit(solution)/shard_map/all_gather | solution.py:338
  52.2 22.8 %all-gather.6.cloned.1.call-done = bf16[512,1280]{1,0:T(8,128)(2,1)} async-done(((bf16[128,1280]{1,0:T(8,128)(2,1)}), bf16[512,1280]{1,0:T(8,128)(2,1)}) %all-gather.6.cloned.1.call-update) | async-done | bytes 1310736 | tf_op jit(solution)/shard_map/all_gather | solution.py:338
  81.9 32.0 %all-gather.8.cloned.1.call-done = bf16[512,1536]{0,1:T(8,128)(2,1)} async-done(((bf16[128,1536]{0,1:T(8,128)(2,1)}), bf16[512,1536]{0,1:T(8,128)(2,1)}) %all-gather.8.cloned.1.call-update) | async-done | bytes 1572880 | tf_op jit(solution)/shard_map/all_gather | solution.py:338
  116.8 2.6 fusion.105
  125.4 36.0 %collective-permute-done.2 = bf16[512,512]{1,0:T(8,128)(2,1)S(1)} collective-permute-done((bf16[512,512]{1,0:T(8,128)(2,1)S(1)}, bf16[512,512]{1,0:T(8,128)(2,1)S(1)}, u32[]{:S(2)}, u32[]{:S(2)}) %collective-permute-start.2) | collective-permute-done | bytes 524320 | tf_op jit(solution)/shard_map/ppermute | solution.py:278
  167.7 6.8 %collective-permute-done.4 = bf16[512,512]{1,0:T(8,128)(2,1)} collective-permute-done((bf16[512,512]{1,0:T(8,128)(2,1)}, bf16[512,512]{1,0:T(8,128)(2,1)}, u32[]{:S(2)}, u32[]{:S(2)}) %collective-permute-start.4) | collective-permute-done | bytes 524320 | tf_op jit(solution)/shard_map/ppermute | solution.py:278
  176.2 2.8 fusion.73
  179.1 2.9 copy.53
  206.4 2.6 collective-permute-start.21
  209.1 2.4 fusion.74
  211.5 5.1 %collective-permute-done.10 = bf16[512,640]{1,0:T(8,128)(2,1)} collective-permute-done((bf16[512,640]{1,0:T(8,128)(2,1)S(1)}, bf16[512,640]{1,0:T(8,128)(2,1)}, u32[]{:S(2)}, u32[]{:S(2)}) %collective-permute-start.10) | collective-permute-done | bytes 655392 | tf_op jit(solution)/shard_map/ppermute | solution.py:278
  216.6 10.9 %fusion.5 = bf16[1024,1536]{1,0:T(8,128)(2,1)S(1)} fusion(bf16[512,640]{1,0:T(8,128)(2,1)} %collective-permute-done.10, bf16[512,640]{1,0:T(8,128)(2,1)} %copy-done.25, bf16[512,768]{1,0:T(8,128)(2,1)S(1)} %copy-done.17, bf16[512,768]{1,0:T(8,128)(2,1)S(1)} %copy-done.16, bf16[512,768]{1,0:T(8,128)(2,1)S(1)} %copy-done.15), kind=kLoop, calls=%fused_computation.7 | loop fusion | flops 23592960 | bytes 6815744 | tf_op jit(solution)/shard_map/concatenate | solution.py:359
  234.8 15.6 %collective-permute-done.13 = bf16[512,768]{0,1:T(8,128)(2,1)S(1)} collective-permute-done((bf16[512,768]{0,1:T(8,128)(2,1)S(1)}, bf16[512,768]{0,1:T(8,128)(2,1)S(1)}, u32[]{:S(2)}, u32[]{:S(2)}) %collective-permute-start.13) | collective-permute-done | bytes 786464 | tf_op jit(solution)/shard_map/ppermute | solution.py:278
  252.7 12.6 %multiply_convert_fusion = (bf16[192,1536]{1,0:T(8,128)(2,1)}, bf16[192,1536]{1,0:T(8,128)(2,1)}, bf16[192,1536]{1,0:T(8,128)(2,1)S(1)}) fusion(f32[192,1536]{1,0:T(8,128)S(1)} %fusion.143, f32[192,1536]{1,0:T(8,128)S(1)} %fusion.66, bf16[192,1024]{1,0:T(8,128)(2,1)S(1)} %copy-done.12, bf16[512,768]{0,1:T(8,128)(2,1)S(1)} %collective-permute-done.14, ...), kind=kOutput, calls=%fused_computation.62 | convolution fusion | flops 620986368 | bytes 7667712 | tf_op jit(solution)/shard_map/dot_general | solution.py:473
  273.1 2.2 collective-permute-done.29
  276.3 11.6 %collective-permute-done.30 = bf16[192,768]{1,0:T(8,128)(2,1)S(1)} collective-permute-done((bf16[192,768]{1,0:T(8,128)(2,1)S(1)}, bf16[192,768]{1,0:T(8,128)(2,1)S(1)}, u32[]{:S(2)}, u32[]{:S(2)}) %collective-permute-start.30) | collective-permute-done | bytes 294944 | tf_op jit(solution)/shard_map/ppermute | solution.py:278
  292.3 3.1 fusion.65
  305.5 4.3 collective-permute-done.40
  309.8 2.9 collective-permute-done.41
  326.5 26.0 %collective-permute-done.24 = bf16[192,512]{1,0:T(8,128)(2,1)S(1)} collective-permute-done((bf16[192,512]{1,0:T(8,128)(2,1)}, bf16[192,512]{1,0:T(8,128)(2,1)S(1)}, u32[]{:S(2)}, u32[]{:S(2)}) %collective-permute-start.24) | collective-permute-done | bytes 196640 | tf_op jit(solution)/shard_map/ppermute | solution.py:278
  355.1 4.5 fusion.6
  380.8 6.1 %collective-permute-done.33 = f32[192,4,128]{2,0,1:T(8,128)S(1)} collective-permute-done((f32[192,4,128]{2,0,1:T(8,128)S(1)}, f32[192,4,128]{2,0,1:T(8,128)S(1)}, u32[]{:S(2)}, u32[]{:S(2)}) %collective-permute-start.33) | collective-permute-done | bytes 393248 | tf_op jit(solution)/shard_map/ppermute | solution.py:278
  391.0 6.6 %collective-permute-done.32 = f32[128,768]{1,0:T(8,128)S(1)} collective-permute-done((f32[128,768]{1,0:T(8,128)}, f32[128,768]{1,0:T(8,128)S(1)}, u32[]{:S(2)}, u32[]{:S(2)}) %collective-permute-start.32) | collective-permute-done | bytes 393248 | tf_op jit(solution)/shard_map/ppermute | solution.py:278
  405.2 12.6 %collective-permute-done.50 = bf16[192,1024]{1,0:T(8,128)(2,1)S(1)} collective-permute-done((bf16[192,1024]{1,0:T(8,128)(2,1)S(1)}, bf16[192,1024]{1,0:T(8,128)(2,1)S(1)}, u32[]{:S(2)}, u32[]{:S(2)}) %collective-permute-start.50) | collective-permute-done | bytes 393248 | tf_op jit(solution)/shard_map/ppermute | solution.py:278
  417.8 2.3 fusion.22
  420.2 2.6 fusion.35
  433.6 15.4 %collective-permute-done.39 = f32[128,1536]{1,0:T(8,128)} collective-permute-done((f32[128,1536]{1,0:T(8,128)}, f32[128,1536]{1,0:T(8,128)}, u32[]{:S(2)}, u32[]{:S(2)}) %collective-permute-start.39) | collective-permute-done | bytes 786464 | tf_op jit(solution)/shard_map/ppermute | solution.py:278
  453.9 2.5 collective-permute-done.46
  457.3 3.0 collective-permute-done.47
  460.7 3.4 reduce-scatter.11.cloned.1.call-done
  469.8 7.7 %collective-permute-done.52 = f32[128,1024]{1,0:T(8,128)S(1)} collective-permute-done((f32[128,1024]{1,0:T(8,128)}, f32[128,1024]{1,0:T(8,128)S(1)}, u32[]{:S(2)}, u32[]{:S(2)}) %collective-permute-start.52) | collective-permute-done | bytes 524320 | tf_op jit(solution)/shard_map/ppermute | solution.py:278
  (511 shorter events, 180.5 us)
Async XLA Ops:
  7.2 33.7 %all-gather.4.cloned.1.call-start = ((), (), s32[]{:S(2)}) async-start(), calls=%async_computation.4 | async-start | bytes 1310720 | tf_op jit(solution)/shard_map/all_gather | solution.py:338
  9.9 65.1 %all-gather.6.cloned.1.call-start = ((), (), s32[]{:S(2)}) async-start(), calls=%async_computation.5 | async-start | bytes 1638400 | tf_op jit(solution)/shard_map/all_gather | solution.py:338
  11.8 102.1 %all-gather.8.cloned.1.call-start = ((), (), s32[]{:S(2)}) async-start(), calls=%async_computation.6 | async-start | bytes 1966080 | tf_op jit(solution)/shard_map/all_gather | solution.py:338
  14.3 33.1 %collective-permute-start.27 = (bf16[192,512]{1,0:T(8,128)(2,1)}, bf16[192,512]{1,0:T(8,128)(2,1)}, u32[]{:S(2)}, u32[]{:S(2)}) collective-permute-start(bf16[192,512]{1,0:T(8,128)(2,1)} %get-tuple-element.137), channel_id=1, source_target_pairs={{0,4},{4,0},{8,12},{12,8},{16,20},{20,16},{24,28},{28,24},{1,5},{5... | collective-permute-start | bytes 589832 | tf_op jit(solution)/shard_map/ppermute | solution.py:278
  17.3 30.1 %collective-permute-start.28 = (bf16[192,512]{1,0:T(8,128)(2,1)}, bf16[192,512]{1,0:T(8,128)(2,1)}, u32[]{:S(2)}, u32[]{:S(2)}) collective-permute-start(bf16[192,512]{1,0:T(8,128)(2,1)} %get-tuple-element.137), channel_id=1, source_target_pairs={{0,6},{2,4},{4,2},{6,0},{8,14},{10,12},{12,10},{14,8},{16,22},{18,... | collective-permute-start | bytes 589832 | tf_op jit(solution)/shard_map/ppermute | solution.py:344
  18.8 28.7 %collective-permute-start.26 = (bf16[192,512]{1,0:T(8,128)(2,1)S(1)}, bf16[192,512]{1,0:T(8,128)(2,1)}, u32[]{:S(2)}, u32[]{:S(2)}) collective-permute-start(bf16[192,512]{1,0:T(8,128)(2,1)S(1)} %get-tuple-element.136), channel_id=1, source_target_pairs={{0,2},{2,0},{1,3},{3,1},{4,6},{6,4},{5,7},{7,5},{8,10},{10,8},{9,1... | collective-permute-start | bytes 589832 | tf_op jit(solution)/shard_map/ppermute | solution.py:278
  19.8 369.4 %reduce-scatter.5.cloned.1.call-start = ((), (), s32[]{:S(2)}) async-start(), calls=%async_computation.7 | async-start | bytes 1966080 | tf_op jit(solution)/shard_map/reduce_scatter | solution.py:379
  40.9 74.6 %collective-permute-start = (bf16[512,1024]{1,0:T(8,128)(2,1)}, bf16[512,1024]{1,0:T(8,128)(2,1)S(1)}, u32[]{:S(2)}, u32[]{:S(2)}) collective-permute-start(bf16[512,1024]{1,0:T(8,128)(2,1)} %all-gather.4.cloned.1.call-done), channel_id=1, source_target_pairs={{0,2},{2,0},{1,3},{3,1},{4,6},{6,4},{5,7},{7,5},{8,10},{10,8},{9,1... | collective-permute-start | bytes 3145736 | tf_op jit(solution)/shard_map/ppermute | solution.py:278
  42.4 77.0 %collective-permute-start.1 = (bf16[512,1024]{1,0:T(8,128)(2,1)}, bf16[512,1024]{1,0:T(8,128)(2,1)}, u32[]{:S(2)}, u32[]{:S(2)}) collective-permute-start(bf16[512,1024]{1,0:T(8,128)(2,1)} %all-gather.4.cloned.1.call-done), channel_id=1, source_target_pairs={{0,4},{4,0},{8,12},{12,8},{16,20},{20,16},{24,28},{28,24},{1,5},{5... | collective-permute-start | bytes 3145736 | tf_op jit(solution)/shard_map/ppermute | solution.py:278
  75.0 111.0 %collective-permute-start.7 = (bf16[512,1280]{1,0:T(8,128)(2,1)}, bf16[512,1280]{1,0:T(8,128)(2,1)}, u32[]{:S(2)}, u32[]{:S(2)}) collective-permute-start(bf16[512,1280]{1,0:T(8,128)(2,1)} %all-gather.6.cloned.1.call-done), channel_id=1, source_target_pairs={{0,4},{4,0},{8,12},{12,8},{16,20},{20,16},{24,28},{28,24},{1,5},{5... | collective-permute-start | bytes 3932168 | tf_op jit(solution)/shard_map/ppermute | solution.py:278
  76.4 112.9 %collective-permute-start.6 = (bf16[512,1280]{1,0:T(8,128)(2,1)}, bf16[512,1280]{1,0:T(8,128)(2,1)}, u32[]{:S(2)}, u32[]{:S(2)}) collective-permute-start(bf16[512,1280]{1,0:T(8,128)(2,1)} %all-gather.6.cloned.1.call-done), channel_id=1, source_target_pairs={{0,2},{2,0},{1,3},{3,1},{4,6},{6,4},{5,7},{7,5},{8,10},{10,8},{9,1... | collective-permute-start | bytes 3932168 | tf_op jit(solution)/shard_map/ppermute | solution.py:278
  113.9 113.6 %collective-permute-start.12 = (bf16[512,1536]{0,1:T(8,128)(2,1)}, bf16[512,1536]{0,1:T(8,128)(2,1)}, u32[]{:S(2)}, u32[]{:S(2)}) collective-permute-start(bf16[512,1536]{0,1:T(8,128)(2,1)} %all-gather.8.cloned.1.call-done), channel_id=1, source_target_pairs={{0,4},{4,0},{8,12},{12,8},{16,20},{20,16},{24,28},{28,24},{1,5},{5... | collective-permute-start | bytes 4718600 | tf_op jit(solution)/shard_map/ppermute | solution.py:278
  116.3 45.0 %collective-permute-start.2 = (bf16[512,512]{1,0:T(8,128)(2,1)S(1)}, bf16[512,512]{1,0:T(8,128)(2,1)S(1)}, u32[]{:S(2)}, u32[]{:S(2)}) collective-permute-start(bf16[512,512]{1,0:T(8,128)(2,1)S(1)} %get-tuple-element.101), channel_id=1, source_target_pairs={{0,4},{4,0},{8,12},{12,8},{16,20},{20,16},{24,28},{28,24},{1,5},{5... | collective-permute-start | bytes 1572872 | tf_op jit(solution)/shard_map/ppermute | solution.py:278
  119.5 111.2 %collective-permute-start.11 = (bf16[512,1536]{0,1:T(8,128)(2,1)}, bf16[512,1536]{0,1:T(8,128)(2,1)}, u32[]{:S(2)}, u32[]{:S(2)}) collective-permute-start(bf16[512,1536]{0,1:T(8,128)(2,1)} %all-gather.8.cloned.1.call-done), channel_id=1, source_target_pairs={{0,2},{2,0},{1,3},{3,1},{4,6},{6,4},{5,7},{7,5},{8,10},{10,8},{9,1... | collective-permute-start | bytes 4718600 | tf_op jit(solution)/shard_map/ppermute | solution.py:278
  174.5 23.8 %collective-permute-start.3 = (bf16[192,4,128]{2,0,1:T(8,128)(2,1)}, bf16[192,4,128]{2,0,1:T(8,128)(2,1)}, u32[]{:S(2)}, u32[]{:S(2)}) collective-permute-start(bf16[192,4,128]{2,0,1:T(8,128)(2,1)} %fusion.72), channel_id=1, source_target_pairs={{0,2},{2,0},{1,3},{3,1},{4,6},{6,4},{5,7},{7,5},{8,10},{10,8},{9,1... | collective-permute-start | bytes 589832 | tf_op jit(solution)/shard_map/ppermute | solution.py:278
  205.5 62.0 %collective-permute-start.19 = (bf16[192,512]{1,0:T(8,128)(2,1)S(1)}, bf16[192,512]{1,0:T(8,128)(2,1)S(1)}, u32[]{:S(2)}, u32[]{:S(2)}) collective-permute-start(bf16[192,512]{1,0:T(8,128)(2,1)S(1)} %get-tuple-element.143), channel_id=1, source_target_pairs={{0,2},{2,0},{1,3},{3,1},{4,6},{6,4},{5,7},{7,5},{8,10},{10,8},{9,1... | collective-permute-start | bytes 589832 | tf_op jit(solution)/shard_map/ppermute | solution.py:278
  206.4 62.5 %collective-permute-start.21 = (bf16[192,512]{1,0:T(8,128)(2,1)S(1)}, bf16[192,512]{1,0:T(8,128)(2,1)S(1)}, u32[]{:S(2)}, u32[]{:S(2)}) collective-permute-start(bf16[192,512]{1,0:T(8,128)(2,1)S(1)} %get-tuple-element.143), channel_id=1, source_target_pairs={{0,6},{2,4},{4,2},{6,0},{8,14},{10,12},{12,10},{14,8},{16,22},{18,... | collective-permute-start | bytes 589832 | tf_op jit(solution)/shard_map/ppermute | solution.py:344
  227.6 41.3 %collective-permute-start.20 = (bf16[192,512]{1,0:T(8,128)(2,1)S(1)}, bf16[192,512]{1,0:T(8,128)(2,1)S(1)}, u32[]{:S(2)}, u32[]{:S(2)}) collective-permute-start(bf16[192,512]{1,0:T(8,128)(2,1)S(1)} %get-tuple-element.142), channel_id=1, source_target_pairs={{0,4},{4,0},{8,12},{12,8},{16,20},{20,16},{24,28},{28,24},{1,5},{5... | collective-permute-start | bytes 589832 | tf_op jit(solution)/shard_map/ppermute | solution.py:278
  230.6 19.7 %collective-permute-start.13 = (bf16[512,768]{0,1:T(8,128)(2,1)S(1)}, bf16[512,768]{0,1:T(8,128)(2,1)S(1)}, u32[]{:S(2)}, u32[]{:S(2)}) collective-permute-start(bf16[512,768]{0,1:T(8,128)(2,1)S(1)} %get-tuple-element.92), channel_id=1, source_target_pairs={{0,2},{2,0},{1,3},{3,1},{4,6},{6,4},{5,7},{7,5},{8,10},{10,8},{9,1... | collective-permute-start | bytes 2359304 | tf_op jit(solution)/shard_map/ppermute | solution.py:278
  232.9 19.7 %collective-permute-start.14 = (bf16[512,768]{0,1:T(8,128)(2,1)S(1)}, bf16[512,768]{0,1:T(8,128)(2,1)S(1)}, u32[]{:S(2)}, u32[]{:S(2)}) collective-permute-start(bf16[512,768]{0,1:T(8,128)(2,1)S(1)} %get-tuple-element.93), channel_id=1, source_target_pairs={{0,4},{4,0},{8,12},{12,8},{16,20},{20,16},{24,28},{28,24},{1,5},{5... | collective-permute-start | bytes 2359304 | tf_op jit(solution)/shard_map/ppermute | solution.py:278
  266.4 21.5 %collective-permute-start.31 = (bf16[192,768]{1,0:T(8,128)(2,1)S(1)}, bf16[192,768]{1,0:T(8,128)(2,1)S(1)}, u32[]{:S(2)}, u32[]{:S(2)}) collective-permute-start(bf16[192,768]{1,0:T(8,128)(2,1)S(1)} %get-tuple-element.117), channel_id=1, source_target_pairs={{0,6},{2,4},{4,2},{6,0},{8,14},{10,12},{12,10},{14,8},{16,22},{18,... | collective-permute-start | bytes 884744 | tf_op jit(solution)/shard_map/ppermute | solution.py:344
  267.5 20.4 %collective-permute-start.30 = (bf16[192,768]{1,0:T(8,128)(2,1)S(1)}, bf16[192,768]{1,0:T(8,128)(2,1)S(1)}, u32[]{:S(2)}, u32[]{:S(2)}) collective-permute-start(bf16[192,768]{1,0:T(8,128)(2,1)S(1)} %get-tuple-element.116), channel_id=1, source_target_pairs={{0,4},{4,0},{8,12},{12,8},{16,20},{20,16},{24,28},{28,24},{1,5},{5... | collective-permute-start | bytes 884744 | tf_op jit(solution)/shard_map/ppermute | solution.py:278
  289.9 133.1 %reduce-scatter.9.cloned.1.call-start = ((), (), s32[]{:S(2)}) async-start(), calls=%async_computation.9 | async-start | bytes 1310720 | tf_op jit(solution)/shard_map/reduce_scatter | solution.py:379
  315.6 112.2 %reduce-scatter.7.cloned.1.call-start = ((), (), s32[]{:S(2)}) async-start(), calls=%async_computation.8 | async-start | bytes 3932160 | tf_op jit(solution)/shard_map/reduce_scatter | solution.py:379
  317.5 37.6 %collective-permute-start.37 = (bf16[192,1536]{1,0:T(8,128)(2,1)S(1)}, bf16[192,1536]{1,0:T(8,128)(2,1)}, u32[]{:S(2)}, u32[]{:S(2)}) collective-permute-start(bf16[192,1536]{1,0:T(8,128)(2,1)S(1)} %pad_maximum_fusion.4), channel_id=1, source_target_pairs={{0,4},{4,0},{8,12},{12,8},{16,20},{20,16},{24,28},{28,24},{1,5},{5... | collective-permute-start | bytes 1769480 | tf_op jit(solution)/shard_map/ppermute | solution.py:278
  318.9 36.2 %collective-permute-start.36 = (bf16[192,1536]{1,0:T(8,128)(2,1)S(1)}, bf16[192,1536]{1,0:T(8,128)(2,1)}, u32[]{:S(2)}, u32[]{:S(2)}) collective-permute-start(bf16[192,1536]{1,0:T(8,128)(2,1)S(1)} %pad_maximum_fusion.5), channel_id=1, source_target_pairs={{0,2},{2,0},{1,3},{3,1},{4,6},{6,4},{5,7},{7,5},{8,10},{10,8},{9,1... | collective-permute-start | bytes 1769480 | tf_op jit(solution)/shard_map/ppermute | solution.py:278
  319.9 35.2 %collective-permute-start.38 = (bf16[192,1536]{1,0:T(8,128)(2,1)S(1)}, bf16[192,1536]{1,0:T(8,128)(2,1)}, u32[]{:S(2)}, u32[]{:S(2)}) collective-permute-start(bf16[192,1536]{1,0:T(8,128)(2,1)S(1)} %pad_maximum_fusion.5), channel_id=1, source_target_pairs={{0,6},{2,4},{4,2},{6,0},{8,14},{10,12},{12,10},{14,8},{16,22},{18,... | collective-permute-start | bytes 1769480 | tf_op jit(solution)/shard_map/ppermute | solution.py:344
  321.2 31.4 %collective-permute-start.24 = (bf16[192,512]{1,0:T(8,128)(2,1)}, bf16[192,512]{1,0:T(8,128)(2,1)S(1)}, u32[]{:S(2)}, u32[]{:S(2)}) collective-permute-start(bf16[192,512]{1,0:T(8,128)(2,1)} %get-tuple-element.139), channel_id=1, source_target_pairs={{0,4},{4,0},{8,12},{12,8},{16,20},{20,16},{24,28},{28,24},{1,5},{5... | collective-permute-start | bytes 589832 | tf_op jit(solution)/shard_map/ppermute | solution.py:278
  324.8 27.7 %collective-permute-start.25 = (bf16[192,512]{1,0:T(8,128)(2,1)}, bf16[192,512]{1,0:T(8,128)(2,1)}, u32[]{:S(2)}, u32[]{:S(2)}) collective-permute-start(bf16[192,512]{1,0:T(8,128)(2,1)} %get-tuple-element.139), channel_id=1, source_target_pairs={{0,6},{2,4},{4,2},{6,0},{8,14},{10,12},{12,10},{14,8},{16,22},{18,... | collective-permute-start | bytes 589832 | tf_op jit(solution)/shard_map/ppermute | solution.py:344
  359.7 104.3 %reduce-scatter.11.cloned.1.call-start = ((), (), s32[]{:S(2)}) async-start(), calls=%async_computation.10 | async-start | bytes 2621440 | tf_op jit(solution)/shard_map/reduce_scatter | solution.py:379
  366.6 20.4 %collective-permute-start.34 = (f32[192,4,128]{0,2,1:T(8,128)}, f32[192,4,128]{0,2,1:T(8,128)}, u32[]{:S(2)}, u32[]{:S(2)}) collective-permute-start(f32[192,4,128]{0,2,1:T(8,128)} %slice.473), channel_id=1, source_target_pairs={{0,2},{2,0},{1,3},{3,1},{4,6},{6,4},{5,7},{7,5},{8,10},{10,8},{9,1... | collective-permute-start | bytes 1179656 | tf_op jit(solution)/shard_map/ppermute | solution.py:278
  427.8 21.1 %collective-permute-start.39 = (f32[128,1536]{1,0:T(8,128)}, f32[128,1536]{1,0:T(8,128)}, u32[]{:S(2)}, u32[]{:S(2)}) collective-permute-start(f32[128,1536]{1,0:T(8,128)} %reduce-scatter.7.cloned.1.call-done), channel_id=1, source_target_pairs={{0,2},{2,0},{1,3},{3,1},{4,6},{6,4},{5,7},{7,5},{8,10},{10,8},{9,1... | collective-permute-start | bytes 2359304 | tf_op jit(solution)/shard_map/ppermute | solution.py:278
  (142 other events, 1691.9 us)
Sparse Core Ops, SparseCore 0:
  10.2 30.6 all-gather.3
  43.0 31.9 all-gather.5
  77.1 36.7 all-gather.7
  290.1 32.7 reduce-scatter.4
  325.0 26.1 reduce-scatter.8
  359.8 57.8 reduce-scatter.6
  420.3 43.6 reduce-scatter.10
